TPU v7x, 128 devices: a whole 4x4x4 slice. The times are simulated.
128 devices in a mesh: facet: 16 (over x, z_hi, core), sub: 4 (over y), wa: 2 (over z_lo).
Axes of the slice: x: 4, y: 4, z: 4 (z_hi: 2, z_lo: 2; z = z_hi * 2 + z_lo), core: 2. Of those that a mesh axis runs over, the one named last changes fastest.
Arguments:
- facets: float32 [16, 512, 2, 4096], P('facet'), may hold values from -6 to 6
- correction: float32 [16, 4096], P('facet'), may hold values from 0.5 to 2
- window: float32 [128], replicated, may hold values from 0.25 to 1
- offsets: int32 [8], replicated, may hold values from 0 to 4095
- phases: float32 [4, 2048], P('wa'), may hold values from -3.140625 to 3.140625
- coverage: int32 [8, 4, 2048], P('sub', 'wa'), may hold values from 0 to 3
Outputs:
- facets_out: float32 [16, 512, 2, 4096], P('facet', ('sub', 'wa'))
All inputs are finite; a program needn't handle non-finite values.
Results may differ from a plain program's by a relative error of at most 0.0001.
Values sent between devices are 32-bit elements; how exact they have to be, the bound alone decides.
No kernel may reach another device: no remote copies, remote signals or barrier semaphores. Data moves between devices by JAX's collectives and lax.ppermute only.
A program may use at most 192 MiB of HBM per device.

v0:
```python
import math

import jax
import jax.numpy as jnp
import numpy as np
from jax import lax
from jax.experimental import pallas as pl
from jax.experimental.pallas import tpu as pltpu
from jax.sharding import PartitionSpec as P

WPLANES = 4
LANES = 128
F32 = jnp.float32
BF16 = jnp.bfloat16


def trig(rows, cols, length):
    product = np.arange(rows, dtype=np.int64)[:, None] * np.arange(cols, dtype=np.int64)[None, :]
    angle = (product % length) * (2.0 * math.pi / length)
    return np.cos(angle), np.sin(angle)


def halves(table):
    high = table.astype(np.float32).astype(BF16)
    low = (table - high.astype(np.float64)).astype(np.float32).astype(BF16)
    return jnp.asarray(high), jnp.asarray(low)


def split(x):
    high = x.astype(BF16)
    return high, (x - high.astype(F32)).astype(BF16)


def mul_const(re, im, c, s):
    tiny = 1e-12
    if abs(s) < tiny:
        return (re, im) if c > 0 else (-re, -im)
    if abs(c) < tiny:
        return (-im, re) if s > 0 else (im, -re)
    if abs(abs(c) - abs(s)) < tiny:
        u = re * c
        v = im * c
        return (u - v, u + v) if c * s > 0 else (u + v, v - u)
    return re * c - im * s, re * s + im * c


def small_fft(re, im, sign):
    n = len(re)
    if n == 1:
        return re, im
    radix = 4 if n % 4 == 0 else 2
    m = n // radix
    parts = [small_fft(re[j::radix], im[j::radix], sign) for j in range(radix)]
    out_re, out_im = [None] * n, [None] * n
    for k in range(m):
        terms = []
        for j in range(radix):
            angle = sign * 2.0 * math.pi * j * k / n
            terms.append(mul_const(parts[j][0][k], parts[j][1][k], math.cos(angle), math.sin(angle)))
        if radix == 2:
            (ar, ai), (br, bi) = terms
            out_re[k], out_im[k] = ar + br, ai + bi
            out_re[k + m], out_im[k + m] = ar - br, ai - bi
        else:
            (ar, ai), (br, bi), (cr, ci), (dr, di) = terms
            sr, si, tr, ti = ar + cr, ai + ci, ar - cr, ai - ci
            ur, ui, vr, vi = br + dr, bi + di, br - dr, bi - di
            out_re[k], out_im[k] = sr + ur, si + ui
            out_re[k + 2 * m], out_im[k + 2 * m] = sr - ur, si - ui
            if sign > 0:
                out_re[k + m], out_im[k + m] = tr - vi, ti + vr
                out_re[k + 3 * m], out_im[k + 3 * m] = tr + vi, ti - vr
            else:
                out_re[k + m], out_im[k + m] = tr + vi, ti - vr
                out_re[k + 3 * m], out_im[k + 3 * m] = tr - vi, ti + vr
    return out_re, out_im


def dot_nt(a, b):
    return lax.dot_general(a, b, (((1,), (1,)), ((), ())), preferred_element_type=F32)


def dot_nn(a, b):
    return lax.dot_general(a, b, (((1,), (0,)), ((), ())), preferred_element_type=F32)


def turned_rows(re, im, part):
    left, right = [], []
    for at in range(0, re.shape[0], part):
        a, b = re[at : at + part], im[at : at + part]
        left += [a, b]
        right += [b, -a]
    return jnp.concatenate([jnp.concatenate(left, 0), jnp.concatenate(right, 0)], 1)


def forward_kernel(
    scal, facets, corr, tw_cos, tw_sin, line_hi, line_lo, block, window, out, xr, xi, yr, yi, spec, sems
):
    rows = xr.shape[0]
    outer = yr.shape[0]
    length = outer * LANES
    half = rows // 2
    groups = rows // 8
    base = pl.multiple_of(scal[0], rows)

    def copies(g):
        at = pl.ds(g * 8, 8)
        return (
            pltpu.make_async_copy(facets.at[pl.ds(base + g * 8, 8), 0, :], xr.at[at, :], sems.at[0, g]),
            pltpu.make_async_copy(facets.at[pl.ds(base + g * 8, 8), 1, :], xi.at[at, :], sems.at[1, g]),
        )

    for g in range(groups):
        for c in copies(g):
            c.start()

    def first(g, carry):
        for c in copies(g):
            c.wait()
        at = pl.ds(pl.multiple_of(g * 8, 8), 8)
        re, im = [], []
        for a in range(outer):
            scale = corr[a : a + 1, :]
            lanes = pl.ds(a * LANES, LANES)
            re.append(xr[at, lanes] * scale)
            im.append(xi[at, lanes] * scale)
        re, im = small_fft(re, im, -1.0)
        for k in range(outer):
            c, s = tw_cos[k : k + 1, :], tw_sin[k : k + 1, :]
            yr[k, at, :] = re[k] * c + im[k] * s
            yi[k, at, :] = im[k] * c - re[k] * s
        return carry

    lax.fori_loop(0, groups, first, 0)

    def second(j, carry):
        both = [turned_rows(yr[2 * j + e], yi[2 * j + e], half) for e in range(2)]
        high, low = split(jnp.concatenate(both, 0))
        z = dot_nt(line_hi[...], high) + dot_nt(line_hi[...], low) + dot_nt(line_lo[...], high)
        for e in range(2):
            spec[pl.ds(2 * j + e, LANES, stride=outer), :] = z[:, e * LANES : (e + 1) * LANES]
        return carry

    lax.fori_loop(0, outer // 2, second, 0)
    spec[length : length + LANES, :] = spec[0:LANES, :]
    table_hi, table_lo = split(block[...] * window[...])
    for s in range(out.shape[0] // 2):
        seg = spec[pl.ds(scal[1 + s], LANES), :]
        high, low = split(seg.T)
        p = dot_nn(high, table_hi) + dot_nn(low, table_hi) + dot_nn(high, table_lo)
        for h in range(2):
            a, b = p[2 * h * half : (2 * h + 1) * half], p[(2 * h + 1) * half : (2 * h + 2) * half]
            out[2 * s + h, 0:half, :] = a[:, :LANES] - b[:, LANES:]
            out[2 * s + h, half : 2 * half, :] = a[:, LANES:] + b[:, :LANES]


def middle_kernel(x, own, other, tw_cos, tw_sin, fwd_hi, fwd_lo, bwd_hi, bwd_lo, out, kc, ks, cnt, br, bi):
    outer = x.shape[0]
    rows = x.shape[1] // 2
    groups = rows // 8
    planes = own.shape[0] // 2
    per = LANES // outer
    lane_i = lax.broadcasted_iota(jnp.int32, (LANES, LANES), 0)
    lane_n = lax.broadcasted_iota(jnp.int32, (LANES, LANES), 1)
    mask = (lane_i // outer) == (lane_n % per)
    spread = (
        lax.broadcasted_iota(jnp.int32, (outer, LANES), 1) // per
        == lax.broadcasted_iota(jnp.int32, (outer, LANES), 0)
    ).astype(F32)
    fold = (
        lax.broadcasted_iota(jnp.int32, (outer, LANES), 1) % outer
        == lax.broadcasted_iota(jnp.int32, (outer, LANES), 0)
    ).astype(F32)
    for src, at in ((own, 0), (other, planes)):
        for w in range(planes):
            wide = dot_nn(src[w].T.astype(BF16), spread.astype(BF16))
            picked = jnp.where(mask, wide, 0.0).astype(BF16)
            cnt[at + w] = dot_nn(fold.astype(BF16), picked)
            kc[at + w] = jnp.cos(src[planes + w])
            ks[at + w] = jnp.sin(src[planes + w])

    out[...] = jnp.zeros(out.shape, F32)

    def plane(w, carry):
        def first(g, c2):
            top = pl.ds(pl.multiple_of(g * 8, 8), 8)
            bot = pl.ds(pl.multiple_of(rows + g * 8, 8), 8)
            re, im = [], []
            for a in range(outer):
                c, s = kc[w, a : a + 1, :], ks[w, a : a + 1, :]
                p, q = x[a, top, :], x[a, bot, :]
                re.append(p * c - q * s)
                im.append(p * s + q * c)
            re, im = small_fft(re, im, -1.0)
            for k in range(outer):
                c, s = tw_cos[k : k + 1, :], tw_sin[k : k + 1, :]
                br[k, top, :] = re[k] * c + im[k] * s
                bi[k, top, :] = im[k] * c - re[k] * s
            return c2

        lax.fori_loop(0, groups, first, 0)
        step = LANES // rows
        for k in range(0, outer, step):
            left = jnp.concatenate([br[k + e] for e in range(step)], 0)
            right = jnp.concatenate([bi[k + e] for e in range(step)], 0)
            high, low = split(jnp.concatenate([left, right], 1))
            g = dot_nn(high, fwd_hi[...]) + dot_nn(low, fwd_hi[...]) + dot_nn(high, fwd_lo[...])
            scaled = []
            for e in range(step):
                row = cnt[w, k + e : k + e + 1, :]
                piece = g[e * rows : (e + 1) * rows]
                scaled.append(jnp.concatenate([piece[:, :LANES] * row, piece[:, LANES:] * row], 1))
            high, low = split(jnp.concatenate(scaled, 0))
            q = dot_nn(high, bwd_hi[...]) + dot_nn(low, bwd_hi[...]) + dot_nn(high, bwd_lo[...])
            for e in range(step):
                c, s = tw_cos[k + e : k + e + 1, :], tw_sin[k + e : k + e + 1, :]
                piece = q[e * rows : (e + 1) * rows]
                re, im = piece[:, :LANES], piece[:, LANES:]
                br[k + e] = re * c - im * s
                bi[k + e] = re * s + im * c

        def last(g, c2):
            top = pl.ds(pl.multiple_of(g * 8, 8), 8)
            bot = pl.ds(pl.multiple_of(rows + g * 8, 8), 8)
            re, im = [], []
            for k in range(outer):
                re.append(br[k, top, :])
                im.append(bi[k, top, :])
            re, im = small_fft(re, im, 1.0)
            for a in range(outer):
                c, s = kc[w, a : a + 1, :], ks[w, a : a + 1, :]
                out[a, top, :] += re[a] * c + im[a] * s
                out[a, bot, :] += im[a] * c - re[a] * s
            return c2

        lax.fori_loop(0, groups, last, 0)
        return carry

    lax.fori_loop(0, 2 * planes, plane, 0)


def backward_kernel(
    scal, x, corr, tw_cos, tw_sin, block, window, line_hi, line_lo, out, acc, yr, yi, zr, zi, sems
):
    rows = zr.shape[0]
    outer = yr.shape[0]
    length = outer * LANES
    half = rows // 2
    groups = rows // 8
    acc[...] = jnp.zeros(acc.shape, F32)
    table_hi, table_lo = split(block[...] * window[...])
    for s in range(x.shape[0] // 2):
        re = jnp.concatenate([x[2 * s, 0:half, :], x[2 * s + 1, 0:half, :]], 0)
        im = jnp.concatenate([x[2 * s, half : 2 * half, :], x[2 * s + 1, half : 2 * half, :]], 0)
        high, low = split(turned_rows(re, im, half))
        z = dot_nt(table_hi, high) + dot_nt(table_hi, low) + dot_nt(table_lo, high)
        at = pl.ds(scal[1 + s], LANES)
        acc[at, :] = acc[at, :] + z
    acc[0:LANES, :] = acc[0:LANES, :] + acc[length : length + LANES, :]

    def second(k, carry):
        z = acc[pl.ds(k, LANES, stride=outer), :]
        high, low = split(z.T)
        p = dot_nn(high, line_hi[...]) + dot_nn(low, line_hi[...]) + dot_nn(high, line_lo[...])
        c, s = tw_cos[pl.ds(k, 1), :], tw_sin[pl.ds(k, 1), :]
        for h in range(2):
            a, b = p[2 * h * half : (2 * h + 1) * half], p[(2 * h + 1) * half : (2 * h + 2) * half]
            re = a[:, :LANES] - b[:, LANES:]
            im = a[:, LANES:] + b[:, :LANES]
            yr[k, h * half : (h + 1) * half, :] = re * c - im * s
            yi[k, h * half : (h + 1) * half, :] = re * s + im * c
        return carry

    lax.fori_loop(0, outer, second, 0)

    def copies(g):
        at = pl.ds(g * 8, 8)
        return (
            pltpu.make_async_copy(zr.at[at, :], out.at[at, 0, :], sems.at[0, g]),
            pltpu.make_async_copy(zi.at[at, :], out.at[at, 1, :], sems.at[1, g]),
        )

    def last(g, carry):
        at = pl.ds(pl.multiple_of(g * 8, 8), 8)
        re, im = [], []
        for k in range(outer):
            re.append(yr[k, at, :])
            im.append(yi[k, at, :])
        re, im = small_fft(re, im, 1.0)
        for a in range(outer):
            scale = corr[a : a + 1, :]
            lanes = pl.ds(a * LANES, LANES)
            zr[at, lanes] = re[a] * scale
            zi[at, lanes] = im[a] * scale
        for c in copies(g):
            c.start()
        return carry

    lax.fori_loop(0, groups, last, 0)
    for g in range(groups):
        for c in copies(g):
            c.wait()


VMEM_LIMIT = 60 * 1024 * 1024


def vmem():
    return pl.BlockSpec(memory_space=pltpu.VMEM)


def hbm():
    return pl.BlockSpec(memory_space=pl.ANY)


def params():
    return pltpu.CompilerParams(vmem_limit_bytes=VMEM_LIMIT)


def on_device(facets, correction, window, offsets, phases, coverage):
    sub_count = lax.axis_size("sub")
    pair_count = lax.axis_size("wa")
    facet_count = lax.axis_size("facet")
    sub = lax.axis_index("sub")
    pair = lax.axis_index("wa")
    facet = lax.axis_index("facet")
    length = facets.shape[3]
    outer = length // LANES
    rows = facets.shape[1] // (sub_count * pair_count)
    half = rows // 2
    per_owner = coverage.shape[0]
    subgrids = offsets.shape[0]
    width = facet_count * LANES

    turned = jnp.roll(offsets.reshape(sub_count, per_owner), -sub, axis=0).reshape(subgrids)
    scal = jnp.concatenate([((sub * pair_count + pair) * rows)[None], turned]).astype(jnp.int32)

    slot = facet // 2
    mine = lax.dynamic_index_in_dim(coverage, slot % per_owner, 0, keepdims=False).astype(F32)
    payload = jnp.concatenate([mine, phases], 0).reshape(-1, facet_count, LANES)
    names = ("facet", "sub", "wa")

    def number(f, y, w):
        return (f * sub_count + y) * pair_count + w

    def fetch(flip):
        route = []
        for f in range(facet_count):
            for y in range(sub_count):
                for w in range(pair_count):
                    source = (f, (y + f // 2 // per_owner) % sub_count, w ^ flip)
                    route.append((number(*source), number(f, y, w)))
        return lax.ppermute(payload, names, route)

    own, other = fetch(0), fetch(1)

    tw = trig(outer, LANES, length)
    tw_cos, tw_sin = jnp.asarray(tw[0], F32), jnp.asarray(tw[1], F32)
    c128, s128 = trig(LANES, LANES, LANES)
    corr = correction.reshape(outer, LANES)
    wide_hi, wide_lo = halves(np.concatenate([c128, s128], 1) * length**-0.5)
    cells = np.concatenate([c128, s128], 1) * LANES**-0.5

    sent = pl.pallas_call(
        forward_kernel,
        grid_spec=pltpu.PrefetchScalarGridSpec(
            num_scalar_prefetch=1,
            grid=(1,),
            in_specs=[hbm()] + [vmem()] * 7,
            out_specs=vmem(),
            scratch_shapes=[
                pltpu.VMEM((rows, length), F32),
                pltpu.VMEM((rows, length), F32),
                pltpu.VMEM((outer, rows, LANES), F32),
                pltpu.VMEM((outer, rows, LANES), F32),
                pltpu.VMEM((length + LANES, LANES), F32),
                pltpu.SemaphoreType.DMA((2, rows // 8)),
            ],
        ),
        out_shape=jax.ShapeDtypeStruct((facet_count, rows, LANES), F32),
        compiler_params=params(),
        name="forward",
    )(
        scal, facets.reshape(facets.shape[1:]), corr, tw_cos, tw_sin, wide_hi, wide_lo,
        jnp.asarray(cells, F32), window.reshape(LANES, 1),
    )
    got = lax.all_to_all(sent, "facet", split_axis=0, concat_axis=0, tiled=True)

    tw2 = trig(facet_count, LANES, width)
    fwd = np.block([[c128, -s128], [s128, c128]])
    fwd_hi, fwd_lo = halves(fwd)
    bwd_hi, bwd_lo = halves(np.block([[c128, s128], [-s128, c128]]) * (1.0 / (width * WPLANES)))
    adjoint = pl.pallas_call(
        middle_kernel,
        in_specs=[vmem()] * 9,
        out_specs=vmem(),
        scratch_shapes=[pltpu.VMEM((WPLANES, facet_count, LANES), F32)] * 3
        + [pltpu.VMEM((facet_count, half, LANES), F32)] * 2,
        out_shape=jax.ShapeDtypeStruct((facet_count, rows, LANES), F32),
        compiler_params=params(),
        name="middle",
    )(
        got, own, other, jnp.asarray(tw2[0], F32), jnp.asarray(tw2[1], F32), fwd_hi, fwd_lo, bwd_hi, bwd_lo
    )
    back = lax.all_to_all(adjoint, "facet", split_axis=0, concat_axis=0, tiled=True)

    result = pl.pallas_call(
        backward_kernel,
        grid_spec=pltpu.PrefetchScalarGridSpec(
            num_scalar_prefetch=1,
            grid=(1,),
            in_specs=[vmem()] * 8,
            out_specs=hbm(),
            scratch_shapes=[
                pltpu.VMEM((length + LANES, LANES), F32),
                pltpu.VMEM((outer, rows, LANES), F32),
                pltpu.VMEM((outer, rows, LANES), F32),
                pltpu.VMEM((rows, length), F32),
                pltpu.VMEM((rows, length), F32),
                pltpu.SemaphoreType.DMA((2, rows // 8)),
            ],
        ),
        out_shape=jax.ShapeDtypeStruct((rows, 2, length), F32),
        compiler_params=params(),
        name="backward",
    )(
        scal, back, corr, tw_cos, tw_sin, jnp.asarray(cells, F32), window.reshape(LANES, 1), wide_hi, wide_lo
    )
    return result.reshape(1, rows, 2, length)


def solution(mesh):
    return jax.shard_map(
        on_device,
        mesh=mesh,
        in_specs=(
            P("facet", None, None, None),
            P("facet", None),
            P(),
            P(),
            P("wa", None),
            P("sub", "wa", None),
        ),
        out_specs=P("facet", ("sub", "wa"), None, None),
        check_vma=False,
    )
```

profile of v0, /device:TPU:1, one launch (start us, length us, event | category | flops | bytes accessed | tf_op | source)
XLA Modules:
  0.0 76.6 jit_solution(18236053498360816836)
XLA Ops:
  0.0 0.0 copy-start.4
  0.0 0.0 copy-start.3
  0.0 0.7 reshape.23
  0.7 0.1 copy.23
  0.8 0.1 pad_add_fusion
  0.9 0.1 constant_dynamic-slice_fusion
  1.0 0.1 copy.25
  1.1 0.1 reshape.24
  1.2 1.4 %copy.26.window = f32[128,1]{1,0:T(8,128)} copy(f32[128,1]{0,1:T(1,128)} %bitcast.17) | data formatting | bytes 1024 | tf_op jit(solution)/shard_map/reshape | solution.py:385
  2.6 0.7 pad_add_fusion.1.scal
  3.2 11.2 %forward.1 = f32[16,64,128]{2,1,0:T(8,128)} custom-call(s32[9]{0:T(128)} %pad_add_fusion.1.scal, f32[512,2,4096]{2,1,0:T(2,128)} %bitcast.12, f32[32,128]{1,0:T(8,128)} %bitcast.13, f32[32,128]{1,0:T(8,128)} %constant.86.clone.tw_cos, f32[32,128]{1,0:T(8,128)} %constant.87.clone.tw_sin, bf16[128,256]{1,0:T(8,128)(2,1)} %constant.88.clone.line_hi, ...), custom_call_target="tpu_custom_call" | custom-call | tf_op jit(solution)/shard_map/forward/pallas_call | solution.py:364
  14.4 9.1 %all-to-all-start = ((f32[16,64,128]{2,1,0:T(8,128)}), f32[16,64,128]{2,1,0:T(8,128)S(1)}, u32[]{:S(2)}, u32[]{:S(2)}) async-start(f32[16,64,128]{2,1,0:T(8,128)} %forward.1), calls=%async_computation | async-start | bytes 1048576 | tf_op jit(solution)/shard_map/all_to_all | solution.py:387
  23.5 0.0 copy-done.4
  23.6 0.0 copy-done.3
  23.6 0.8 %collective-permute-start.1 = (f32[4,16,128]{2,1,0:T(8,128)S(1)}, f32[4,16,128]{2,1,0:T(8,128)S(1)}, u32[]{:S(2)}, u32[]{:S(2)}) collective-permute-start(f32[4,16,128]{2,1,0:T(8,128)S(1)} %bitcast.15), channel_id=1, source_target_pairs={{1,0},{0,1},{3,2},{2,3},{5,4},{4,5},{7,6},{6,7},{9,8},{8,9},{11,10... | collective-permute-start | bytes 98312 | tf_op jit(solution)/shard_map/ppermute | solution.py:353
  24.4 0.7 collective-permute-start
  25.1 2.5 %collective-permute-done.1.other = f32[4,16,128]{2,1,0:T(8,128)S(1)} collective-permute-done((f32[4,16,128]{2,1,0:T(8,128)S(1)}, f32[4,16,128]{2,1,0:T(8,128)S(1)}, u32[]{:S(2)}, u32[]{:S(2)}) %collective-permute-start.1) | collective-permute-done | bytes 32800 | tf_op jit(solution)/shard_map/ppermute | solution.py:353
  27.6 0.0 copy-start.1
  27.6 0.0 collective-permute-done.own
  27.6 0.0 copy-start.2
  27.6 7.1 %all-to-all-done.x = f32[16,64,128]{2,1,0:T(8,128)S(1)} async-done(((f32[16,64,128]{2,1,0:T(8,128)}), f32[16,64,128]{2,1,0:T(8,128)S(1)}, u32[]{:S(2)}, u32[]{:S(2)}) %all-to-all-start) | async-done | bytes 524320 | tf_op jit(solution)/shard_map/all_to_all | solution.py:387
  34.7 0.0 copy-done.1
  34.7 0.0 copy-done.2
  34.7 0.0 copy-start
  34.7 0.8 %copy-done = f32[16,64,128]{2,1,0:T(8,128)} copy-done((f32[16,64,128]{2,1,0:T(8,128)}, f32[16,64,128]{2,1,0:T(8,128)S(1)}, u32[]{:S(2)}) %copy-start) | copy-done | bytes 524312
  35.5 7.4 %middle.1 = f32[16,64,128]{2,1,0:T(8,128)} custom-call(f32[16,64,128]{2,1,0:T(8,128)} %copy-done, f32[4,16,128]{2,1,0:T(8,128)} %copy-done.2, f32[4,16,128]{2,1,0:T(8,128)} %copy-done.1, f32[16,128]{1,0:T(8,128)} %constant.95.clone.tw_cos, f32[16,128]{1,0:T(8,128)} %constant.96.clone.tw_sin, bf16[256,256]{1,0:T(8,128)(2,1)} %constant.91.clone.fwd_hi, ...), custom_call_target="tpu_custom_call" | custom-call | tf_op jit(solution)/shard_map/middle/pallas_call | solution.py:393
  43.0 19.6 %all_to_all.10.x = f32[16,64,128]{2,1,0:T(8,128)} all-to-all(f32[16,64,128]{2,1,0:T(8,128)} %middle.1), channel_id=1, replica_groups=mesh['facet'=16,'sub'=4,'wa'=2] {'facet'}, dimensions={0} | all-to-all | bytes 1048576 | tf_op jit(solution)/shard_map/all_to_all | solution.py:405
  62.6 14.0 %backward.1 = f32[64,2,4096]{2,1,0:T(2,128)} custom-call(s32[9]{0:T(128)} %pad_add_fusion.1.scal, f32[16,64,128]{2,1,0:T(8,128)} %all_to_all.10.x, f32[32,128]{1,0:T(8,128)} %bitcast.14, f32[32,128]{1,0:T(8,128)} %constant.86.clone.tw_cos, f32[32,128]{1,0:T(8,128)} %constant.87.clone.tw_sin, f32[128,256]{1,0:T(8,128)} %constant.90.clone.block, ...), custom_call_target="tpu_custom_call" | custom-call | tf_op jit(solution)/shard_map/backward/pallas_call | solution.py:407
  (3 shorter events, 0.0 us)
Async XLA Ops:
  0.0 23.5 %copy-start.4 = (s32[2,2,2048]{2,1,0:T(2,128)S(1)}, s32[2,2,2048]{2,1,0:T(2,128)}, u32[]{:S(2)}) copy-start(s32[2,2,2048]{2,1,0:T(2,128)} %param.23) | copy-start | bytes 98308
  0.0 23.6 %copy-start.3 = (f32[2,2048]{1,0:T(2,128)S(1)}, f32[2,2048]{1,0:T(2,128)}, u32[]{:S(2)}) copy-start(f32[2,2048]{1,0:T(2,128)} %param.22) | copy-start | bytes 49156
  14.4 20.3 %all-to-all-start = ((f32[16,64,128]{2,1,0:T(8,128)}), f32[16,64,128]{2,1,0:T(8,128)S(1)}, u32[]{:S(2)}, u32[]{:S(2)}) async-start(f32[16,64,128]{2,1,0:T(8,128)} %forward.1), calls=%async_computation | async-start | bytes 1048576 | tf_op jit(solution)/shard_map/all_to_all | solution.py:387
  23.6 4.0 %collective-permute-start.1 = (f32[4,16,128]{2,1,0:T(8,128)S(1)}, f32[4,16,128]{2,1,0:T(8,128)S(1)}, u32[]{:S(2)}, u32[]{:S(2)}) collective-permute-start(f32[4,16,128]{2,1,0:T(8,128)S(1)} %bitcast.15), channel_id=1, source_target_pairs={{1,0},{0,1},{3,2},{2,3},{5,4},{4,5},{7,6},{6,7},{9,8},{8,9},{11,10... | collective-permute-start | bytes 98312 | tf_op jit(solution)/shard_map/ppermute | solution.py:353
  24.4 3.2 %collective-permute-start = (f32[4,16,128]{2,1,0:T(8,128)S(1)}, f32[4,16,128]{2,1,0:T(8,128)S(1)}, u32[]{:S(2)}, u32[]{:S(2)}) collective-permute-start(f32[4,16,128]{2,1,0:T(8,128)S(1)} %bitcast.16), channel_id=1, source_target_pairs={{0,0},{1,1},{2,2},{3,3},{4,4},{5,5},{6,6},{7,7},{8,8},{9,9},{10,10... | collective-permute-start | bytes 98312 | tf_op jit(solution)/shard_map/ppermute | solution.py:353
  27.6 7.1 %copy-start.1 = (f32[4,16,128]{2,1,0:T(8,128)}, f32[4,16,128]{2,1,0:T(8,128)S(1)}, u32[]{:S(2)}) copy-start(f32[4,16,128]{2,1,0:T(8,128)S(1)} %collective-permute-done.1.other) | copy-start | bytes 98308
  27.6 7.1 %copy-start.2 = (f32[4,16,128]{2,1,0:T(8,128)}, f32[4,16,128]{2,1,0:T(8,128)S(1)}, u32[]{:S(2)}) copy-start(f32[4,16,128]{2,1,0:T(8,128)S(1)} %collective-permute-done.own) | copy-start | bytes 98308
  34.7 0.8 %copy-start = (f32[16,64,128]{2,1,0:T(8,128)}, f32[16,64,128]{2,1,0:T(8,128)S(1)}, u32[]{:S(2)}) copy-start(f32[16,64,128]{2,1,0:T(8,128)S(1)} %all-to-all-done.x) | copy-start | bytes 1572868
where the time goes:
time: 77.1 us; the launch traced here: 76.6 us
  Pallas kernels  32.6 us (42%)
  blocking collectives  19.6 us (25%)
  starting transfers between devices  10.6 us (14%)
  waiting for transfers between devices  9.66 us (13%)
  local copies, waits for them, and re-layouts  3.29 us (4%)
    all_to_all x1, blocking collectives, on_device(): lax.all_to_all(adjoint, 'facet', split_axis=0, concat_axis=0, tiled=True)  19.6 us
    pallas_call x1, Pallas kernels, on_device(): pl.pallas_call(backward_kernel, grid_spec=pltpu.PrefetchScalarGridSpec(nu...  14 us
    pallas_call x1, Pallas kernels, on_device(): pl.pallas_call(forward_kernel, grid_spec=pltpu.PrefetchScalarGridSpec(num...  11.2 us
    all_to_all x1, starting transfers between devices, on_device(): got = lax.all_to_all(sent, 'facet', split_axis=0, concat_axis=0, tiled=True)  9.13 us
    pallas_call x1, Pallas kernels, on_device(): pl.pallas_call(middle_kernel, in_specs=[vmem()] * 9, out_specs=vmem(), sc...  7.44 us
    all_to_all x1, waiting for transfers between devices, on_device(): got = lax.all_to_all(sent, 'facet', split_axis=0, concat_axis=0, tiled=True)  7.13 us
    ppermute x2, waiting for transfers between devices, fetch(): return lax.ppermute(payload, names, route)  2.53 us
  transfers between devices with their start and end apart: 3, of which 2 were waited for; matrix products, arithmetic and copies ran while one was open for 0% of the time, Pallas kernels for 0%

commit v1 on v0

v1 whole, which is shorter than its diff:
```python
import math

import jax
import jax.numpy as jnp
import numpy as np
from jax import lax
from jax.experimental import pallas as pl
from jax.experimental.pallas import tpu as pltpu
from jax.sharding import PartitionSpec as P

WPLANES = 4
LANES = 128
F32 = jnp.float32
BF16 = jnp.bfloat16


def trig(rows, cols, length):
    product = np.arange(rows, dtype=np.int64)[:, None] * np.arange(cols, dtype=np.int64)[None, :]
    angle = (product % length) * (2.0 * math.pi / length)
    return np.cos(angle), np.sin(angle)


def np_halves(table):
    high = table.astype(np.float32).astype(BF16)
    low = (table - high.astype(np.float64)).astype(np.float32).astype(BF16)
    return high, low


def halves(table):
    high, low = np_halves(table)
    return jnp.asarray(high), jnp.asarray(low)


def split(x):
    high = x.astype(BF16)
    return high, (x - high.astype(F32)).astype(BF16)


def mul_const(re, im, c, s):
    tiny = 1e-12
    if abs(s) < tiny:
        return (re, im) if c > 0 else (-re, -im)
    if abs(c) < tiny:
        return (-im, re) if s > 0 else (im, -re)
    if abs(abs(c) - abs(s)) < tiny:
        u = re * c
        v = im * c
        return (u - v, u + v) if c * s > 0 else (u + v, v - u)
    return re * c - im * s, re * s + im * c


def small_fft(re, im, sign):
    n = len(re)
    if n == 1:
        return re, im
    radix = 4 if n % 4 == 0 else 2
    m = n // radix
    parts = [small_fft(re[j::radix], im[j::radix], sign) for j in range(radix)]
    out_re, out_im = [None] * n, [None] * n
    for k in range(m):
        terms = []
        for j in range(radix):
            angle = sign * 2.0 * math.pi * j * k / n
            terms.append(mul_const(parts[j][0][k], parts[j][1][k], math.cos(angle), math.sin(angle)))
        if radix == 2:
            (ar, ai), (br, bi) = terms
            out_re[k], out_im[k] = ar + br, ai + bi
            out_re[k + m], out_im[k + m] = ar - br, ai - bi
        else:
            (ar, ai), (br, bi), (cr, ci), (dr, di) = terms
            sr, si, tr, ti = ar + cr, ai + ci, ar - cr, ai - ci
            ur, ui, vr, vi = br + dr, bi + di, br - dr, bi - di
            out_re[k], out_im[k] = sr + ur, si + ui
            out_re[k + 2 * m], out_im[k + 2 * m] = sr - ur, si - ui
            if sign > 0:
                out_re[k + m], out_im[k + m] = tr - vi, ti + vr
                out_re[k + 3 * m], out_im[k + 3 * m] = tr + vi, ti - vr
            else:
                out_re[k + m], out_im[k + m] = tr + vi, ti - vr
                out_re[k + 3 * m], out_im[k + 3 * m] = tr - vi, ti + vr
    return out_re, out_im


def dot_nt(a, b):
    return lax.dot_general(a, b, (((1,), (1,)), ((), ())), preferred_element_type=F32)


def dot_nn(a, b):
    return lax.dot_general(a, b, (((1,), (0,)), ((), ())), preferred_element_type=F32)


def product(x, table_hi, table_lo):
    high, low = split(x)
    return dot_nn(high, table_hi) + dot_nn(low, table_hi) + dot_nn(high, table_lo)


def turned_rows(re, im, half):
    left, right = [], []
    for at in range(0, re.shape[0], half):
        a, b = re[at : at + half], im[at : at + half]
        left += [a, b]
        right += [b, -a]
    return jnp.concatenate([jnp.concatenate(left, 0), jnp.concatenate(right, 0)], 1)


def turned_halves(pairs, half):
    highs, lows = [], []
    for re, im in pairs:
        (rh, rl), (ih, il) = split(re), split(im)
        highs.append(turned_rows(rh, ih, half))
        lows.append(turned_rows(rl, il, half))
    return jnp.concatenate(highs, 0), jnp.concatenate(lows, 0)


def columns_product(table, table_hi, pairs, half):
    high, low = turned_halves(pairs, half)
    n = table_hi.shape[0]
    both = dot_nt(table, high)
    return both[:n] + both[n:] + dot_nt(table_hi, low)


def side_by_side(x, half):
    re = [x[at : at + half] for at in range(0, x.shape[0], 2 * half)]
    im = [x[at + half : at + 2 * half] for at in range(0, x.shape[0], 2 * half)]
    return jnp.concatenate([jnp.concatenate(re, 0), jnp.concatenate(im, 0)], 1)


PITCH = LANES + 16
FRONT = 8


def piece_row(offset, c, outer):
    at = offset + c
    shift = outer.bit_length() - 1
    return (at & (outer - 1)) * PITCH + (at >> shift) + FRONT


def window_column(window, outer):
    per = LANES // outer
    row = lax.broadcasted_iota(jnp.int32, (LANES, LANES), 0)
    lane = lax.broadcasted_iota(jnp.int32, (LANES, LANES), 1)
    wide = jnp.broadcast_to(window, (LANES, LANES))
    return jnp.sum(jnp.where(lane == row // per + outer * (row % per), wide, 0.0), axis=1, keepdims=True)


def slot_offset(offsets, slot, subs, per_owner):
    owner = (slot // per_owner + lax.axis_index("sub")) & (subs - 1)
    return offsets[owner * per_owner + slot % per_owner]


def forward_kernel(
    subs, pairs, per_owner, offsets, facets, corr_h, tw_h, line_h, block_h, window_h, out, xr, xi, yr, yi, spec, corr, tw, line,
    block, window, sems, table_sems
):
    rows = xr.shape[0]
    outer = yr.shape[0]
    half = rows // 2
    groups = rows // 8
    base = pl.multiple_of((lax.axis_index("sub") * pairs + lax.axis_index("wa")) * rows, rows)

    def copies(g):
        at = pl.ds(g * 8, 8)
        return (
            pltpu.make_async_copy(facets.at[pl.ds(base + g * 8, 8), 0, :], xr.at[at, :], sems.at[0, g]),
            pltpu.make_async_copy(facets.at[pl.ds(base + g * 8, 8), 1, :], xi.at[at, :], sems.at[1, g]),
        )

    pieces = ((corr_h, corr), (tw_h, tw), (line_h, line), (block_h, block), (window_h, window))
    tables = [pltpu.make_async_copy(src, dst, table_sems.at[i]) for i, (src, dst) in enumerate(pieces)]
    for c in tables[:2]:
        c.start()
    for g in range(groups):
        for c in copies(g):
            c.start()
    for c in tables[2:]:
        c.start()
    for c in tables[:2]:
        c.wait()

    def first(g, carry):
        for c in copies(g):
            c.wait()
        at = pl.ds(pl.multiple_of(g * 8, 8), 8)
        re, im = [], []
        for a in range(outer):
            scale = corr[a : a + 1, :]
            lanes = pl.ds(a * LANES, LANES)
            re.append(xr[at, lanes] * scale)
            im.append(xi[at, lanes] * scale)
        re, im = small_fft(re, im, -1.0)
        for k in range(outer):
            c, s = tw[k : k + 1, :], tw[outer + k : outer + k + 1, :]
            yr[k, at, :] = re[k] * c + im[k] * s
            yi[k, at, :] = im[k] * c - re[k] * s
        return carry

    lax.fori_loop(0, groups, first, 0)
    for c in tables[2:]:
        c.wait()

    def second(j, carry):
        z = columns_product(line[...], line[:LANES, :], [(yr[2 * j + e], yi[2 * j + e]) for e in range(2)], half)
        for e in range(2):
            at = pl.multiple_of((2 * j + e) * PITCH + FRONT, 8)
            spec[pl.ds(at, LANES), :] = z[:, e * LANES : (e + 1) * LANES]
            spec[pl.ds(at + LANES, 8), :] = z[0:8, e * LANES : (e + 1) * LANES]
        return carry

    lax.fori_loop(0, outer // 2, second, 0, unroll=2)
    top = block[...] * window_column(window[...], outer)
    bottom = jnp.concatenate([-top[:, LANES:], top[:, :LANES]], 1)
    table_hi, table_lo = split(jnp.concatenate([top, bottom], 0))
    near = lax.broadcasted_iota(jnp.int32, (8, LANES), 0) < 4
    slots = out.shape[0] // 2
    batch = 4
    for first_slot in range(0, slots, batch):
        stacked = []
        for slot in range(first_slot, first_slot + batch):
            offset = slot_offset(offsets, slot, subs, per_owner)
            pieces = []
            for c in range(0, outer, 2):
                even = spec[pl.ds(piece_row(offset, c, outer), 8), :]
                odd = spec[pl.ds(piece_row(offset, c + 1, outer) - 4, 8), :]
                pieces.append(jnp.where(near, even, odd))
            stacked.append(side_by_side(jnp.concatenate(pieces, 0).T, half))
        p = product(jnp.concatenate(stacked, 0), table_hi, table_lo)
        for e in range(batch):
            for h in range(2):
                at = (2 * e + h) * half
                out[2 * (first_slot + e) + h, 0:half, :] = p[at : at + half, :LANES]
                out[2 * (first_slot + e) + h, half : 2 * half, :] = p[at : at + half, LANES:]


def ready_kernel(own, other, out):
    planes, outer = own.shape[0] // 2, own.shape[1]
    per = LANES // outer
    row = lax.broadcasted_iota(jnp.int32, (LANES, LANES), 0)
    lane = lax.broadcasted_iota(jnp.int32, (LANES, LANES), 1)
    mask = (row // outer) == (lane % per)
    short_row = lax.broadcasted_iota(jnp.int32, (outer, LANES), 0)
    short_lane = lax.broadcasted_iota(jnp.int32, (outer, LANES), 1)
    spread = (short_lane // per == short_row).astype(F32).astype(BF16)
    fold = (short_lane % outer == short_row).astype(F32).astype(BF16)
    for src, at in ((own, 0), (other, planes)):
        for w in range(planes):
            wide = dot_nn(src[w].T.astype(BF16), spread)
            out[2, at + w] = dot_nn(fold, jnp.where(mask, wide, 0.0).astype(BF16))
            out[0, at + w] = jnp.cos(src[planes + w])
            out[1, at + w] = jnp.sin(src[planes + w])


def middle_kernel(x, ready, tw_cos, tw_sin, fwd_hi, fwd_lo, bwd_hi, bwd_lo, out, br, bi, qr, qi):
    outer = x.shape[0]
    rows = x.shape[1] // 2
    groups = rows // 8
    planes = ready.shape[1]
    parts = 2
    step = outer // parts

    def first(w, g):
        top, bot = slice(g * 8, g * 8 + 8), slice(rows + g * 8, rows + g * 8 + 8)
        re, im = [], []
        for a in range(outer):
            c, s = ready[0, w, a : a + 1, :], ready[1, w, a : a + 1, :]
            p, q = x[a, top, :], x[a, bot, :]
            re.append(p * c - q * s)
            im.append(p * s + q * c)
        re, im = small_fft(re, im, -1.0)
        for k in range(outer):
            c, s = tw_cos[k : k + 1, :], tw_sin[k : k + 1, :]
            br[w % 2, k, top, :] = re[k] * c + im[k] * s
            bi[w % 2, k, top, :] = im[k] * c - re[k] * s

    def last(w, g):
        top, bot = slice(g * 8, g * 8 + 8), slice(rows + g * 8, rows + g * 8 + 8)
        re = [qr[w % 2, k, top, :] for k in range(outer)]
        im = [qi[w % 2, k, top, :] for k in range(outer)]
        re, im = small_fft(re, im, 1.0)
        for a in range(outer):
            c, s = ready[0, w, a : a + 1, :], ready[1, w, a : a + 1, :]
            hr, hi = re[a] * c + im[a] * s, im[a] * c - re[a] * s
            if w == 0:
                out[a, top, :] = hr
                out[a, bot, :] = hi
            else:
                out[a, top, :] += hr
                out[a, bot, :] += hi

    def to_grid(w, part):
        at = range(part * step, (part + 1) * step)
        left = jnp.concatenate([br[w % 2, k] for k in at], 0)
        right = jnp.concatenate([bi[w % 2, k] for k in at], 0)
        return product(jnp.concatenate([left, right], 1), fwd_hi[...], fwd_lo[...])

    def from_grid(w, part, g):
        scaled = []
        for e in range(step):
            row = ready[2, w, part * step + e : part * step + e + 1, :]
            piece = g[e * rows : (e + 1) * rows]
            scaled.append(jnp.concatenate([piece[:, :LANES] * row, piece[:, LANES:] * row], 1))
        q = product(jnp.concatenate(scaled, 0), bwd_hi[...], bwd_lo[...])
        for e in range(step):
            k = part * step + e
            c, s = tw_cos[k : k + 1, :], tw_sin[k : k + 1, :]
            re, im = q[e * rows : (e + 1) * rows, :LANES], q[e * rows : (e + 1) * rows, LANES:]
            qr[w % 2, k] = re * c - im * s
            qi[w % 2, k] = re * s + im * c

    for g in range(groups):
        first(0, g)
    for w in range(planes):
        for part in range(parts):
            grid = to_grid(w, part)
            for g in range(part * groups // parts, (part + 1) * groups // parts):
                if w + 1 < planes:
                    first(w + 1, g)
            from_grid(w, part, grid)
            for g in range(part * groups // parts, (part + 1) * groups // parts):
                if w > 0:
                    last(w - 1, g)
    for g in range(groups):
        last(planes - 1, g)


def backward_kernel(
    subs, per_owner, offsets, x, corr, tw_cos, tw_sin, block, window, line_hi, line_lo, out, acc, yr, yi, zr, zi, sems
):
    rows = zr.shape[0]
    outer = yr.shape[0]
    half = rows // 2
    groups = rows // 8
    acc[...] = jnp.zeros(acc.shape, F32)
    table_hi, table_lo = split(block[...] * window_column(window[...], outer))
    table = jnp.concatenate([table_hi, table_lo], 0)
    near = lax.broadcasted_iota(jnp.int32, (8, LANES), 0) < 4
    slots = x.shape[0] // 2
    for first_slot in range(0, slots, 2):
        parts = []
        for slot in range(first_slot, first_slot + 2):
            re = jnp.concatenate([x[2 * slot, 0:half, :], x[2 * slot + 1, 0:half, :]], 0)
            im = jnp.concatenate([x[2 * slot, half : 2 * half, :], x[2 * slot + 1, half : 2 * half, :]], 0)
            parts.append((re, im))
        z = columns_product(table, table_hi, parts, half)
        for e in range(2):
            offset = slot_offset(offsets, first_slot + e, subs, per_owner)
            at, value = [], []
            for c in range(outer):
                block_rows = z[(c // 2) * 8 : (c // 2) * 8 + 8, e * LANES : (e + 1) * LANES]
                at.append(pl.ds(piece_row(offset, c, outer) - (c % 2) * 4, 8))
                keep = near if c % 2 == 0 else jnp.logical_not(near)
                value.append(acc[at[c], :] + jnp.where(keep, block_rows, 0.0))
            for c in range(outer):
                acc[at[c], :] = value[c]

    batch = 4

    def second(j, carry):
        stacked = []
        for e in range(batch):
            at = pl.multiple_of((batch * j + e) * PITCH + FRONT, 8)
            head = acc[pl.ds(at, 8), :] + acc[pl.ds(at + LANES, 8), :]
            z = jnp.concatenate([head, acc[pl.ds(at + 8, LANES - 8), :]], 0)
            stacked.append(side_by_side(z.T, half))
        p = product(jnp.concatenate(stacked, 0), line_hi[...], line_lo[...])
        for e in range(batch):
            k = batch * j + e
            c, s = tw_cos[pl.ds(k, 1), :], tw_sin[pl.ds(k, 1), :]
            re, im = p[e * rows : (e + 1) * rows, :LANES], p[e * rows : (e + 1) * rows, LANES:]
            yr[k] = re * c - im * s
            yi[k] = re * s + im * c
        return carry

    lax.fori_loop(0, outer // batch, second, 0)

    def copies(g):
        at = pl.ds(g * 8, 8)
        return (
            pltpu.make_async_copy(zr.at[at, :], out.at[at, 0, :], sems.at[0, g]),
            pltpu.make_async_copy(zi.at[at, :], out.at[at, 1, :], sems.at[1, g]),
        )

    def last(g, carry):
        at = pl.ds(pl.multiple_of(g * 8, 8), 8)
        re, im = [], []
        for k in range(outer):
            re.append(yr[k, at, :])
            im.append(yi[k, at, :])
        re, im = small_fft(re, im, 1.0)
        for a in range(outer):
            scale = corr[a : a + 1, :]
            lanes = pl.ds(a * LANES, LANES)
            zr[at, lanes] = re[a] * scale
            zi[at, lanes] = im[a] * scale
        for c in copies(g):
            c.start()
        return carry

    lax.fori_loop(0, groups, last, 0)
    for g in range(groups):
        for c in copies(g):
            c.wait()


MIB = 1024 * 1024


def vmem():
    return pl.BlockSpec(memory_space=pltpu.VMEM)


def hbm():
    return pl.BlockSpec(memory_space=pltpu.HBM)


def smem():
    return pl.BlockSpec(memory_space=pltpu.SMEM)


def params(mib):
    return pltpu.CompilerParams(vmem_limit_bytes=mib * MIB)


def cost(flops, nbytes):
    return pl.CostEstimate(flops=flops, bytes_accessed=nbytes, transcendentals=0)


def on_device(facets, correction, window, offsets, phases, coverage):
    sub_count = lax.axis_size("sub")
    pair_count = lax.axis_size("wa")
    facet_count = lax.axis_size("facet")
    facet = lax.axis_index("facet")
    length = facets.shape[3]
    outer = length // LANES
    rows = facets.shape[1] // (sub_count * pair_count)
    half = rows // 2
    per_owner = coverage.shape[0]
    width = facet_count * LANES


    slot = facet // 2
    mine = lax.dynamic_index_in_dim(coverage, slot % per_owner, 0, keepdims=False).astype(F32)
    payload = jnp.concatenate([mine, phases], 0).reshape(-1, facet_count, LANES)
    names = ("facet", "sub", "wa")

    def number(f, y, w):
        return (f * sub_count + y) * pair_count + w

    def fetch(flip):
        route = []
        for f in range(facet_count):
            for y in range(sub_count):
                for w in range(pair_count):
                    source = (f, (y + f // 2 // per_owner) % sub_count, w ^ flip)
                    route.append((number(*source), number(f, y, w)))
        return lax.ppermute(payload, names, route)

    own, other = fetch(0), fetch(1)
    ready = pl.pallas_call(
        ready_kernel,
        in_specs=[vmem()] * 2,
        out_specs=vmem(),
        out_shape=jax.ShapeDtypeStruct((3, WPLANES, facet_count, LANES), F32),
        compiler_params=params(4),
        cost_estimate=cost(10**7, 10**6),
        name="ready",
    )(own, other)

    tw = trig(outer, LANES, length)
    tw_cos, tw_sin = jnp.asarray(tw[0], F32), jnp.asarray(tw[1], F32)
    tw_both = jnp.asarray(np.concatenate(tw, 0), F32)
    c128, s128 = trig(LANES, LANES, LANES)
    corr = correction.reshape(outer, LANES)
    line = jnp.asarray(np.concatenate(np_halves(np.concatenate([c128, s128], 1) * length**-0.5), 0))
    per = LANES // outer
    order = np.array([m // per + outer * (m % per) for m in range(LANES)])
    block = jnp.asarray(np.concatenate([c128[order], s128[order]], 1) * LANES**-0.5, F32)
    window = window.reshape(1, LANES)

    sent = pl.pallas_call(
        lambda *refs: forward_kernel(sub_count, pair_count, per_owner, *refs),
        in_specs=[smem()] + [hbm()] * 6,
        out_specs=vmem(),
        scratch_shapes=[
            pltpu.VMEM((rows, length), F32),
            pltpu.VMEM((rows, length), F32),
            pltpu.VMEM((outer, rows, LANES), F32),
            pltpu.VMEM((outer, rows, LANES), F32),
            pltpu.VMEM((outer * PITCH, LANES), F32),
            pltpu.VMEM(corr.shape, F32),
            pltpu.VMEM((2 * outer, LANES), F32),
            pltpu.VMEM(line.shape, BF16),
            pltpu.VMEM(block.shape, F32),
            pltpu.VMEM(window.shape, F32),
            pltpu.SemaphoreType.DMA((2, rows // 8)),
            pltpu.SemaphoreType.DMA((5,)),
        ],
        out_shape=jax.ShapeDtypeStruct((facet_count, rows, LANES), F32),
        compiler_params=params(60),
        cost_estimate=cost(10**9, 10**7),
        name="forward",
    )(offsets, facets.reshape(facets.shape[1:]), corr, tw_both, line, block, window)
    got = lax.all_to_all(sent, "facet", split_axis=0, concat_axis=0, tiled=True)

    tw2 = trig(facet_count, LANES, width)
    fwd_hi, fwd_lo = halves(np.block([[c128, -s128], [s128, c128]]))
    inverse = np.block([[c128, s128], [-s128, c128]])
    bwd_hi, bwd_lo = halves(inverse * (1.0 / (width * WPLANES)))
    adjoint = pl.pallas_call(
        middle_kernel,
        in_specs=[vmem()] * 8,
        out_specs=vmem(),
        scratch_shapes=[pltpu.VMEM((2, facet_count, half, LANES), F32)] * 4,
        out_shape=jax.ShapeDtypeStruct((facet_count, rows, LANES), F32),
        compiler_params=params(12),
        cost_estimate=cost(10**9, 10**7),
        name="middle",
    )(got, ready, jnp.asarray(tw2[0], F32), jnp.asarray(tw2[1], F32), fwd_hi, fwd_lo, bwd_hi, bwd_lo)
    back = lax.all_to_all(adjoint, "facet", split_axis=0, concat_axis=0, tiled=True)

    line_hi, line_lo = halves(inverse * length**-0.5)
    result = pl.pallas_call(
        lambda *refs: backward_kernel(sub_count, per_owner, *refs),
        in_specs=[smem()] + [vmem()] * 8,
        out_specs=hbm(),
        scratch_shapes=[
            pltpu.VMEM((outer * PITCH, LANES), F32),
            pltpu.VMEM((outer, rows, LANES), F32),
            pltpu.VMEM((outer, rows, LANES), F32),
            pltpu.VMEM((rows, length), F32),
            pltpu.VMEM((rows, length), F32),
            pltpu.SemaphoreType.DMA((2, rows // 8)),
        ],
        out_shape=jax.ShapeDtypeStruct((rows, 2, length), F32),
        compiler_params=params(16),
        cost_estimate=cost(10**9, 10**7),
        name="backward",
    )(offsets, back, corr, tw_cos, tw_sin, block, window, line_hi, line_lo)
    return result.reshape(1, rows, 2, length)


def solution(mesh):
    return jax.shard_map(
        on_device,
        mesh=mesh,
        in_specs=(
            P("facet", None, None, None),
            P("facet", None),
            P(),
            P(),
            P("wa", None),
            P("sub", "wa", None),
        ),
        out_specs=P("facet", ("sub", "wa"), None, None),
        check_vma=False,
    )
```

time: 77.1 us -> 56.4 us (0.73)
  Pallas kernels: 32.6 us -> 16.7 us
  local copies, waits for them, and re-layouts: 3.29 us -> 0.09 us
    pallas_call x3 -> x4, Pallas kernels: 32.6 us -> 16.7 us  [the longest x1 7.02 us: on_device(): pl.pallas_call(lambda *refs: forward_kernel(sub_count, pair_count, per_ow...]
    reshape x4 -> x0, local copies, waits for them, and re-layouts: 2.31 us -> none  [the longest x1 1.39 us: on_device(): window.reshape(LANES, 1)]
  transfers between devices with their start and end apart: 3 -> 3, of which waited for: 2 -> 2; matrix products, arithmetic and copies ran while one was open for 0% -> 0% of each run, Pallas kernels for 0% -> 1%
where the time goes in v1:
time: 56.4 us; the launch traced here: 56.1 us
  blocking collectives  19.1 us (34%)
  Pallas kernels  16.7 us (30%)
  starting transfers between devices  10.6 us (19%)
  waiting for transfers between devices  9.26 us (16%)
    all_to_all x1, blocking collectives, on_device(): lax.all_to_all(adjoint, 'facet', split_axis=0, concat_axis=0, tiled=True)  19.1 us
    all_to_all x1, starting transfers between devices, on_device(): got = lax.all_to_all(sent, 'facet', split_axis=0, concat_axis=0, tiled=True)  9.12 us
    pallas_call x1, Pallas kernels, on_device(): pl.pallas_call(lambda *refs: forward_kernel(sub_count, pair_count, per_ow...  7.02 us
    all_to_all x1, waiting for transfers between devices, on_device(): got = lax.all_to_all(sent, 'facet', split_axis=0, concat_axis=0, tiled=True)  6.72 us
    pallas_call x1, Pallas kernels, on_device(): pl.pallas_call(lambda *refs: backward_kernel(sub_count, per_owner, *refs)...  6.11 us
    pallas_call x1, Pallas kernels, on_device(): pl.pallas_call(middle_kernel, in_specs=[vmem()] * 8, out_specs=vmem(), sc...  3.19 us
    ppermute x2, waiting for transfers between devices, fetch(): return lax.ppermute(payload, names, route)  2.53 us
    ppermute x2, starting transfers between devices, fetch(): return lax.ppermute(payload, names, route)  1.46 us
  transfers between devices with their start and end apart: 3, of which 2 were waited for; matrix products, arithmetic and copies ran while one was open for 0% of the time, Pallas kernels for 1%

profile of v1, /device:TPU:1, one launch (start us, length us, event | category | flops | bytes accessed | tf_op | source)
XLA Modules:
  0.0 56.1 jit_solution(15746422488889700479)
XLA Ops:
  0.0 0.0 copy-start
  0.0 0.0 copy-start.12
  0.0 0.0 copy-start.13
  0.0 0.0 copy-start.6
  0.0 0.0 copy-start.7
  0.0 0.0 copy-start.8
  0.0 0.0 copy-start.9
  0.1 0.0 copy-start.4
  0.1 0.0 copy-start.5
  0.1 0.0 copy-start.10
  0.1 0.0 copy-start.11
  0.1 0.0 copy-start.2
  0.1 0.0 copy-start.3
  0.1 0.0 copy-start.1
  0.1 0.0 copy-start.15
  0.2 0.0 copy-start.14
  0.2 7.0 %forward.1 = f32[16,64,128]{2,1,0:T(8,128)} custom-call(s32[8]{0:T(128)} %refs_0_.3, f32[512,2,4096]{2,1,0:T(2,128)} %bitcast.15, f32[32,128]{1,0:T(8,128)} %bitcast.11, f32[64,128]{1,0:T(8,128)} %constant.62.clone.refs_3_, bf16[256,256]{1,0:T(8,128)(2,1)} %constant.63.clone.refs_4_, f32[128,256]{1,0:T(8,128)} %constant.64.clone.refs_5_, f32[1,128]{1,0:T(1,128)} %bitcast.13), custom_call_target="tpu_custom_call" | custom-call | flops 1000000000 | bytes 10000000 | tf_op jit(solution)/shard_map/forward/pallas_call | solution.py:479
  7.2 9.1 %all-to-all-start = ((f32[16,64,128]{2,1,0:T(8,128)}), f32[16,64,128]{2,1,0:T(8,128)S(1)}, u32[]{:S(2)}, u32[]{:S(2)}) async-start(f32[16,64,128]{2,1,0:T(8,128)} %forward.1), calls=%async_computation | async-start | bytes 1048576 | tf_op jit(solution)/shard_map/all_to_all | solution.py:502
  16.3 0.0 copy-done.15
  16.3 0.0 copy-done.14
  16.4 0.8 %collective-permute-start.1 = (f32[4,16,128]{2,1,0:T(8,128)S(1)}, f32[4,16,128]{2,1,0:T(8,128)S(1)}, u32[]{:S(2)}, u32[]{:S(2)}) collective-permute-start(f32[4,16,128]{2,1,0:T(8,128)S(1)} %bitcast.16), channel_id=1, source_target_pairs={{1,0},{0,1},{3,2},{2,3},{5,4},{4,5},{7,6},{6,7},{9,8},{8,9},{11,10... | collective-permute-start | bytes 98312 | tf_op jit(solution)/shard_map/ppermute | solution.py:455
  17.2 0.7 %collective-permute-start = (f32[4,16,128]{2,1,0:T(8,128)S(1)}, f32[4,16,128]{2,1,0:T(8,128)S(1)}, u32[]{:S(2)}, u32[]{:S(2)}) collective-permute-start(f32[4,16,128]{2,1,0:T(8,128)S(1)} %bitcast.17), channel_id=1, source_target_pairs={{0,0},{1,1},{2,2},{3,3},{4,4},{5,5},{6,6},{7,7},{8,8},{9,9},{10,10... | collective-permute-start | bytes 98312 | tf_op jit(solution)/shard_map/ppermute | solution.py:455
  17.9 2.5 %collective-permute-done.1.other = f32[4,16,128]{2,1,0:T(8,128)S(1)} collective-permute-done((f32[4,16,128]{2,1,0:T(8,128)S(1)}, f32[4,16,128]{2,1,0:T(8,128)S(1)}, u32[]{:S(2)}, u32[]{:S(2)}) %collective-permute-start.1) | collective-permute-done | bytes 32800 | tf_op jit(solution)/shard_map/ppermute | solution.py:455
  20.4 0.0 collective-permute-done.own
  20.4 0.4 ready.1
  20.8 6.7 %all-to-all-done.x = f32[16,64,128]{2,1,0:T(8,128)S(1)} async-done(((f32[16,64,128]{2,1,0:T(8,128)}), f32[16,64,128]{2,1,0:T(8,128)S(1)}, u32[]{:S(2)}, u32[]{:S(2)}) %all-to-all-start) | async-done | bytes 524320 | tf_op jit(solution)/shard_map/all_to_all | solution.py:502
  27.5 0.0 copy-done.12
  27.5 0.0 copy-done.13
  27.5 0.0 copy-done.6
  27.5 0.0 copy-done.7
  27.5 0.0 copy-done.8
  27.5 0.0 copy-done.9
  27.6 3.2 %middle.1 = f32[16,64,128]{2,1,0:T(8,128)S(1)} custom-call(f32[16,64,128]{2,1,0:T(8,128)S(1)} %all-to-all-done.x, f32[3,4,16,128]{3,2,1,0:T(8,128)S(1)} %ready.1, f32[16,128]{1,0:T(8,128)S(1)} %copy-done.13, f32[16,128]{1,0:T(8,128)S(1)} %copy-done.12, bf16[256,256]{1,0:T(8,128)(2,1)S(1)} %copy-done.9, bf16[256,256]{1,0:T(8,128)(2,1)S(1)} %copy-done.8, ...), custom_call_target="tpu_custom_call" | custom-call | flops 1000000000 | bytes 10000000 | tf_op jit(solution)/shard_map/middle/pallas_call | solution.py:508
  30.8 19.1 %all_to_all.10.refs_1_ = f32[16,64,128]{2,1,0:T(8,128)S(1)} all-to-all(f32[16,64,128]{2,1,0:T(8,128)S(1)} %middle.1), channel_id=1, replica_groups=mesh['facet'=16,'sub'=4,'wa'=2] {'facet'}, dimensions={0} | all-to-all | bytes 1048576 | tf_op jit(solution)/shard_map/all_to_all | solution.py:518
  49.9 0.0 copy-done
  49.9 0.0 copy-done.4
  49.9 0.0 copy-done.5
  49.9 0.0 copy-done.10
  49.9 0.0 copy-done.11
  49.9 0.0 copy-done.2
  49.9 0.0 copy-done.3
  50.0 0.0 copy-done.1
  50.0 6.1 %backward.1 = f32[64,2,4096]{2,1,0:T(2,128)} custom-call(s32[8]{0:T(128)S(1)} %copy-done.2, f32[16,64,128]{2,1,0:T(8,128)S(1)} %all_to_all.10.refs_1_, f32[32,128]{1,0:T(8,128)S(1)} %bitcast.12, f32[32,128]{1,0:T(8,128)S(1)} %copy-done.11, f32[32,128]{1,0:T(8,128)S(1)} %copy-done.10, f32[128,256]{1,0:T(8,128)S(1)} %copy-done, f32[1,128]{1,0:T(1,128)S(1)} %bitcast.14, ...), custom_call_target="tpu_custom_call" | custom-call | flops 1000000000 | bytes 10000000 | tf_op jit(solution)/shard_map/backward/pallas_call | solution.py:521
  (3 shorter events, 0.0 us)
Async XLA Ops:
  0.0 49.9 %copy-start = (f32[128,256]{1,0:T(8,128)S(1)}, f32[128,256]{1,0:T(8,128)}, u32[]{:S(2)}) copy-start(f32[128,256]{1,0:T(8,128)} %constant.64.clone.refs_5_) | copy-start | bytes 393220
  0.0 27.5 %copy-start.12 = (f32[16,128]{1,0:T(8,128)S(1)}, f32[16,128]{1,0:T(8,128)}, u32[]{:S(2)}) copy-start(f32[16,128]{1,0:T(8,128)} %constant.70.clone.tw_sin) | copy-start | bytes 24580
  0.0 27.5 %copy-start.13 = (f32[16,128]{1,0:T(8,128)S(1)}, f32[16,128]{1,0:T(8,128)}, u32[]{:S(2)}) copy-start(f32[16,128]{1,0:T(8,128)} %constant.69.clone.tw_cos) | copy-start | bytes 24580
  0.0 27.5 %copy-start.6 = (bf16[256,256]{1,0:T(8,128)(2,1)S(1)}, bf16[256,256]{1,0:T(8,128)(2,1)}, u32[]{:S(2)}) copy-start(bf16[256,256]{1,0:T(8,128)(2,1)} %constant.68.clone.bwd_lo) | copy-start | bytes 393220
  0.0 27.5 %copy-start.7 = (bf16[256,256]{1,0:T(8,128)(2,1)S(1)}, bf16[256,256]{1,0:T(8,128)(2,1)}, u32[]{:S(2)}) copy-start(bf16[256,256]{1,0:T(8,128)(2,1)} %constant.67.clone.bwd_hi) | copy-start | bytes 393220
  0.0 27.5 %copy-start.8 = (bf16[256,256]{1,0:T(8,128)(2,1)S(1)}, bf16[256,256]{1,0:T(8,128)(2,1)}, u32[]{:S(2)}) copy-start(bf16[256,256]{1,0:T(8,128)(2,1)} %constant.66.clone.fwd_lo) | copy-start | bytes 393220
  0.0 27.5 %copy-start.9 = (bf16[256,256]{1,0:T(8,128)(2,1)S(1)}, bf16[256,256]{1,0:T(8,128)(2,1)}, u32[]{:S(2)}) copy-start(bf16[256,256]{1,0:T(8,128)(2,1)} %constant.65.clone.fwd_hi) | copy-start | bytes 393220
  0.1 49.8 %copy-start.4 = (bf16[256,256]{1,0:T(8,128)(2,1)S(1)}, bf16[256,256]{1,0:T(8,128)(2,1)}, u32[]{:S(2)}) copy-start(bf16[256,256]{1,0:T(8,128)(2,1)} %constant.72.clone.refs_8_) | copy-start | bytes 393220
  0.1 49.8 %copy-start.5 = (bf16[256,256]{1,0:T(8,128)(2,1)S(1)}, bf16[256,256]{1,0:T(8,128)(2,1)}, u32[]{:S(2)}) copy-start(bf16[256,256]{1,0:T(8,128)(2,1)} %constant.71.clone.refs_7_) | copy-start | bytes 393220
  0.1 49.8 %copy-start.10 = (f32[32,128]{1,0:T(8,128)S(1)}, f32[32,128]{1,0:T(8,128)}, u32[]{:S(2)}) copy-start(f32[32,128]{1,0:T(8,128)} %constant.61.clone.refs_4_) | copy-start | bytes 49156
  0.1 49.8 %copy-start.11 = (f32[32,128]{1,0:T(8,128)S(1)}, f32[32,128]{1,0:T(8,128)}, u32[]{:S(2)}) copy-start(f32[32,128]{1,0:T(8,128)} %constant.60.clone.refs_3_) | copy-start | bytes 49156
  0.1 49.8 %copy-start.2 = (s32[8]{0:T(128)S(1)}, s32[8]{0:T(128)}, u32[]{:S(2)}) copy-start(s32[8]{0:T(128)} %refs_0_.3) | copy-start | bytes 100
  0.1 49.8 %copy-start.3 = (f32[128]{0:T(128)S(1)}, f32[128]{0:T(128)}, u32[]{:S(2)}) copy-start(f32[128]{0:T(128)} %param.21) | copy-start | bytes 1540
  0.1 49.8 %copy-start.1 = (f32[1,4096]{1,0:T(1,128)S(1)}, f32[1,4096]{1,0:T(1,128)}, u32[]{:S(2)}) copy-start(f32[1,4096]{1,0:T(1,128)} %param.20) | copy-start | bytes 49156
  0.1 16.2 %copy-start.15 = (s32[2,2,2048]{2,1,0:T(2,128)S(1)}, s32[2,2,2048]{2,1,0:T(2,128)}, u32[]{:S(2)}) copy-start(s32[2,2,2048]{2,1,0:T(2,128)} %param.24) | copy-start | bytes 98308
  0.2 16.2 %copy-start.14 = (f32[2,2048]{1,0:T(2,128)S(1)}, f32[2,2048]{1,0:T(2,128)}, u32[]{:S(2)}) copy-start(f32[2,2048]{1,0:T(2,128)} %param.23) | copy-start | bytes 49156
  7.2 20.3 %all-to-all-start = ((f32[16,64,128]{2,1,0:T(8,128)}), f32[16,64,128]{2,1,0:T(8,128)S(1)}, u32[]{:S(2)}, u32[]{:S(2)}) async-start(f32[16,64,128]{2,1,0:T(8,128)} %forward.1), calls=%async_computation | async-start | bytes 1048576 | tf_op jit(solution)/shard_map/all_to_all | solution.py:502
  16.4 4.0 %collective-permute-start.1 = (f32[4,16,128]{2,1,0:T(8,128)S(1)}, f32[4,16,128]{2,1,0:T(8,128)S(1)}, u32[]{:S(2)}, u32[]{:S(2)}) collective-permute-start(f32[4,16,128]{2,1,0:T(8,128)S(1)} %bitcast.16), channel_id=1, source_target_pairs={{1,0},{0,1},{3,2},{2,3},{5,4},{4,5},{7,6},{6,7},{9,8},{8,9},{11,10... | collective-permute-start | bytes 98312 | tf_op jit(solution)/shard_map/ppermute | solution.py:455
  17.2 3.2 %collective-permute-start = (f32[4,16,128]{2,1,0:T(8,128)S(1)}, f32[4,16,128]{2,1,0:T(8,128)S(1)}, u32[]{:S(2)}, u32[]{:S(2)}) collective-permute-start(f32[4,16,128]{2,1,0:T(8,128)S(1)} %bitcast.17), channel_id=1, source_target_pairs={{0,0},{1,1},{2,2},{3,3},{4,4},{5,5},{6,6},{7,7},{8,8},{9,9},{10,10... | collective-permute-start | bytes 98312 | tf_op jit(solution)/shard_map/ppermute | solution.py:455

commit v2 on v1

--- a/solution.py
+++ b/solution.py
@@ -445,16 +445,14 @@
     def number(f, y, w):
         return (f * sub_count + y) * pair_count + w
 
-    def fetch(flip):
-        route = []
-        for f in range(facet_count):
-            for y in range(sub_count):
-                for w in range(pair_count):
-                    source = (f, (y + f // 2 // per_owner) % sub_count, w ^ flip)
-                    route.append((number(*source), number(f, y, w)))
-        return lax.ppermute(payload, names, route)
-
-    own, other = fetch(0), fetch(1)
+    route = []
+    for f in range(facet_count):
+        for y in range(sub_count):
+            for w in range(pair_count):
+                source = (f, (y + f // 2 // per_owner) % sub_count, w ^ (f % 2))
+                route.append((number(*source), number(f, y, w)))
+    fetched = lax.ppermute(payload, names, route)
+    swapped = lax.ppermute(fetched, "facet", [(f, f ^ 1) for f in range(facet_count)])
     ready = pl.pallas_call(
         ready_kernel,
         in_specs=[vmem()] * 2,
@@ -463,7 +461,7 @@
         compiler_params=params(4),
         cost_estimate=cost(10**7, 10**6),
         name="ready",
-    )(own, other)
+    )(fetched, swapped)
 
     tw = trig(outer, LANES, length)
     tw_cos, tw_sin = jnp.asarray(tw[0], F32), jnp.asarray(tw[1], F32)

time: 56.4 us -> 53.4 us (0.947)
  blocking collectives: 19.1 us -> 16.2 us
  starting transfers between devices: 10.6 us -> 11.8 us
  waiting for transfers between devices: 9.26 us -> 8.06 us
    all_to_all x1, blocking collectives: 19.1 us -> 16.2 us  [on_device(): lax.all_to_all(adjoint, 'facet', split_axis=0, concat_axis=0, tiled=True)]
    all_to_all x1, waiting for transfers between devices: 6.72 us -> 3.86 us  [on_device(): got = lax.all_to_all(sent, 'facet', split_axis=0, concat_axis=0, tiled=True)]
    ppermute x2, waiting for transfers between devices: 2.53 us -> 4.2 us  [the longest x1 3 us: on_device(): fetched = lax.ppermute(payload, names, route)]
    ppermute x2, starting transfers between devices: 1.46 us -> 2.65 us  [the longest x1 2.65 us: on_device(): fetched = lax.ppermute(payload, names, route)]
  transfers between devices with their start and end apart: 3 -> 3, of which waited for: 2 -> 3; matrix products, arithmetic and copies ran while one was open for 0% -> 0% of each run, Pallas kernels for 1% -> 1%
where the time goes in v2:
time: 53.4 us; the launch traced here: 53.1 us
  Pallas kernels  16.7 us (31%)
  blocking collectives  16.2 us (30%)
  starting transfers between devices  11.8 us (22%)
  waiting for transfers between devices  8.06 us (15%)
    all_to_all x1, blocking collectives, on_device(): lax.all_to_all(adjoint, 'facet', split_axis=0, concat_axis=0, tiled=True)  16.2 us
    all_to_all x1, starting transfers between devices, on_device(): got = lax.all_to_all(sent, 'facet', split_axis=0, concat_axis=0, tiled=True)  9.12 us
    pallas_call x1, Pallas kernels, on_device(): pl.pallas_call(lambda *refs: forward_kernel(sub_count, pair_count, per_ow...  7.02 us
    pallas_call x1, Pallas kernels, on_device(): pl.pallas_call(lambda *refs: backward_kernel(sub_count, per_owner, *refs)...  6.11 us
    all_to_all x1, waiting for transfers between devices, on_device(): got = lax.all_to_all(sent, 'facet', split_axis=0, concat_axis=0, tiled=True)  3.86 us
    pallas_call x1, Pallas kernels, on_device(): pl.pallas_call(middle_kernel, in_specs=[vmem()] * 8, out_specs=vmem(), sc...  3.19 us
    ppermute x1, waiting for transfers between devices, on_device(): fetched = lax.ppermute(payload, names, route)  3 us
    ppermute x1, starting transfers between devices, on_device(): fetched = lax.ppermute(payload, names, route)  2.65 us
  transfers between devices with their start and end apart: 3, of which 3 were waited for; matrix products, arithmetic and copies ran while one was open for 0% of the time, Pallas kernels for 1%

profile of v2, /device:TPU:1, one launch (start us, length us, event | category | flops | bytes accessed | tf_op | source)
XLA Modules:
  0.0 53.1 jit_solution(7351817873747681738)
XLA Ops:
  0.0 0.0 copy-start
  0.0 0.0 copy-start.12
  0.0 0.0 copy-start.13
  0.0 0.0 copy-start.6
  0.0 0.0 copy-start.7
  0.0 0.0 copy-start.8
  0.0 0.0 copy-start.9
  0.1 0.0 copy-start.4
  0.1 0.0 copy-start.5
  0.1 0.0 copy-start.10
  0.1 0.0 copy-start.11
  0.1 0.0 copy-start.2
  0.1 0.0 copy-start.3
  0.1 0.0 copy-start.1
  0.1 0.0 copy-start.15
  0.2 0.0 copy-start.14
  0.2 7.0 %forward.1 = f32[16,64,128]{2,1,0:T(8,128)} custom-call(s32[8]{0:T(128)} %refs_0_.3, f32[512,2,4096]{2,1,0:T(2,128)} %bitcast.15, f32[32,128]{1,0:T(8,128)} %bitcast.11, f32[64,128]{1,0:T(8,128)} %constant.62.clone.refs_3_, bf16[256,256]{1,0:T(8,128)(2,1)} %constant.63.clone.refs_4_, f32[128,256]{1,0:T(8,128)} %constant.64.clone.refs_5_, f32[1,128]{1,0:T(1,128)} %bitcast.13), custom_call_target="tpu_custom_call" | custom-call | flops 1000000000 | bytes 10000000 | tf_op jit(solution)/shard_map/forward/pallas_call | solution.py:477
  7.2 9.1 %all-to-all-start = ((f32[16,64,128]{2,1,0:T(8,128)}), f32[16,64,128]{2,1,0:T(8,128)S(1)}, u32[]{:S(2)}, u32[]{:S(2)}) async-start(f32[16,64,128]{2,1,0:T(8,128)} %forward.1), calls=%async_computation | async-start | bytes 1048576 | tf_op jit(solution)/shard_map/all_to_all | solution.py:500
  16.3 0.0 copy-done.15
  16.3 0.0 copy-done.14
  16.4 2.7 %collective-permute-start = (f32[4,16,128]{2,1,0:T(8,128)S(1)}, f32[4,16,128]{2,1,0:T(8,128)S(1)}, u32[]{:S(2)}, u32[]{:S(2)}) collective-permute-start(f32[4,16,128]{2,1,0:T(8,128)S(1)} %bitcast.16), channel_id=1, source_target_pairs={{0,0},{1,1},{2,2},{3,3},{4,4},{5,5},{6,6},{7,7},{9,8},{8,9},{11,10... | collective-permute-start | bytes 98312 | tf_op jit(solution)/shard_map/ppermute | solution.py:454
  19.0 3.0 %collective-permute-done.own = f32[4,16,128]{2,1,0:T(8,128)S(1)} collective-permute-done((f32[4,16,128]{2,1,0:T(8,128)S(1)}, f32[4,16,128]{2,1,0:T(8,128)S(1)}, u32[]{:S(2)}, u32[]{:S(2)}) %collective-permute-start) | collective-permute-done | bytes 32800 | tf_op jit(solution)/shard_map/ppermute | solution.py:454
  22.0 0.0 collective-permute-start.1
  22.0 1.2 %collective-permute-done.1.other = f32[4,16,128]{2,1,0:T(8,128)S(1)} collective-permute-done((f32[4,16,128]{2,1,0:T(8,128)S(1)}, f32[4,16,128]{2,1,0:T(8,128)S(1)}, u32[]{:S(2)}, u32[]{:S(2)}) %collective-permute-start.1) | collective-permute-done | bytes 32800 | tf_op jit(solution)/shard_map/ppermute | solution.py:455
  23.3 0.4 ready.1
  23.7 3.9 %all-to-all-done.x = f32[16,64,128]{2,1,0:T(8,128)S(1)} async-done(((f32[16,64,128]{2,1,0:T(8,128)}), f32[16,64,128]{2,1,0:T(8,128)S(1)}, u32[]{:S(2)}, u32[]{:S(2)}) %all-to-all-start) | async-done | bytes 524320 | tf_op jit(solution)/shard_map/all_to_all | solution.py:500
  27.5 0.0 copy-done.12
  27.5 0.0 copy-done.13
  27.5 0.0 copy-done.6
  27.5 0.0 copy-done.7
  27.5 0.0 copy-done.8
  27.5 0.0 copy-done.9
  27.6 3.2 %middle.1 = f32[16,64,128]{2,1,0:T(8,128)S(1)} custom-call(f32[16,64,128]{2,1,0:T(8,128)S(1)} %all-to-all-done.x, f32[3,4,16,128]{3,2,1,0:T(8,128)S(1)} %ready.1, f32[16,128]{1,0:T(8,128)S(1)} %copy-done.13, f32[16,128]{1,0:T(8,128)S(1)} %copy-done.12, bf16[256,256]{1,0:T(8,128)(2,1)S(1)} %copy-done.9, bf16[256,256]{1,0:T(8,128)(2,1)S(1)} %copy-done.8, ...), custom_call_target="tpu_custom_call" | custom-call | flops 1000000000 | bytes 10000000 | tf_op jit(solution)/shard_map/middle/pallas_call | solution.py:506
  30.8 16.2 %all_to_all.10.refs_1_ = f32[16,64,128]{2,1,0:T(8,128)S(1)} all-to-all(f32[16,64,128]{2,1,0:T(8,128)S(1)} %middle.1), channel_id=1, replica_groups=mesh['facet'=16,'sub'=4,'wa'=2] {'facet'}, dimensions={0} | all-to-all | bytes 1048576 | tf_op jit(solution)/shard_map/all_to_all | solution.py:516
  46.9 0.0 copy-done
  46.9 0.0 copy-done.4
  46.9 0.0 copy-done.5
  46.9 0.0 copy-done.10
  47.0 0.0 copy-done.11
  47.0 0.0 copy-done.2
  47.0 0.0 copy-done.3
  47.0 0.0 copy-done.1
  47.0 6.1 %backward.1 = f32[64,2,4096]{2,1,0:T(2,128)} custom-call(s32[8]{0:T(128)S(1)} %copy-done.2, f32[16,64,128]{2,1,0:T(8,128)S(1)} %all_to_all.10.refs_1_, f32[32,128]{1,0:T(8,128)S(1)} %bitcast.12, f32[32,128]{1,0:T(8,128)S(1)} %copy-done.11, f32[32,128]{1,0:T(8,128)S(1)} %copy-done.10, f32[128,256]{1,0:T(8,128)S(1)} %copy-done, f32[1,128]{1,0:T(1,128)S(1)} %bitcast.14, ...), custom_call_target="tpu_custom_call" | custom-call | flops 1000000000 | bytes 10000000 | tf_op jit(solution)/shard_map/backward/pallas_call | solution.py:519
  (3 shorter events, 0.0 us)
Async XLA Ops:
  0.0 46.9 %copy-start = (f32[128,256]{1,0:T(8,128)S(1)}, f32[128,256]{1,0:T(8,128)}, u32[]{:S(2)}) copy-start(f32[128,256]{1,0:T(8,128)} %constant.64.clone.refs_5_) | copy-start | bytes 393220
  0.0 27.5 %copy-start.12 = (f32[16,128]{1,0:T(8,128)S(1)}, f32[16,128]{1,0:T(8,128)}, u32[]{:S(2)}) copy-start(f32[16,128]{1,0:T(8,128)} %constant.70.clone.tw_sin) | copy-start | bytes 24580
  0.0 27.5 %copy-start.13 = (f32[16,128]{1,0:T(8,128)S(1)}, f32[16,128]{1,0:T(8,128)}, u32[]{:S(2)}) copy-start(f32[16,128]{1,0:T(8,128)} %constant.69.clone.tw_cos) | copy-start | bytes 24580
  0.0 27.5 %copy-start.6 = (bf16[256,256]{1,0:T(8,128)(2,1)S(1)}, bf16[256,256]{1,0:T(8,128)(2,1)}, u32[]{:S(2)}) copy-start(bf16[256,256]{1,0:T(8,128)(2,1)} %constant.68.clone.bwd_lo) | copy-start | bytes 393220
  0.0 27.5 %copy-start.7 = (bf16[256,256]{1,0:T(8,128)(2,1)S(1)}, bf16[256,256]{1,0:T(8,128)(2,1)}, u32[]{:S(2)}) copy-start(bf16[256,256]{1,0:T(8,128)(2,1)} %constant.67.clone.bwd_hi) | copy-start | bytes 393220
  0.0 27.5 %copy-start.8 = (bf16[256,256]{1,0:T(8,128)(2,1)S(1)}, bf16[256,256]{1,0:T(8,128)(2,1)}, u32[]{:S(2)}) copy-start(bf16[256,256]{1,0:T(8,128)(2,1)} %constant.66.clone.fwd_lo) | copy-start | bytes 393220
  0.0 27.5 %copy-start.9 = (bf16[256,256]{1,0:T(8,128)(2,1)S(1)}, bf16[256,256]{1,0:T(8,128)(2,1)}, u32[]{:S(2)}) copy-start(bf16[256,256]{1,0:T(8,128)(2,1)} %constant.65.clone.fwd_hi) | copy-start | bytes 393220
  0.1 46.9 %copy-start.4 = (bf16[256,256]{1,0:T(8,128)(2,1)S(1)}, bf16[256,256]{1,0:T(8,128)(2,1)}, u32[]{:S(2)}) copy-start(bf16[256,256]{1,0:T(8,128)(2,1)} %constant.72.clone.refs_8_) | copy-start | bytes 393220
  0.1 46.9 %copy-start.5 = (bf16[256,256]{1,0:T(8,128)(2,1)S(1)}, bf16[256,256]{1,0:T(8,128)(2,1)}, u32[]{:S(2)}) copy-start(bf16[256,256]{1,0:T(8,128)(2,1)} %constant.71.clone.refs_7_) | copy-start | bytes 393220
  0.1 46.9 %copy-start.10 = (f32[32,128]{1,0:T(8,128)S(1)}, f32[32,128]{1,0:T(8,128)}, u32[]{:S(2)}) copy-start(f32[32,128]{1,0:T(8,128)} %constant.61.clone.refs_4_) | copy-start | bytes 49156
  0.1 46.9 %copy-start.11 = (f32[32,128]{1,0:T(8,128)S(1)}, f32[32,128]{1,0:T(8,128)}, u32[]{:S(2)}) copy-start(f32[32,128]{1,0:T(8,128)} %constant.60.clone.refs_3_) | copy-start | bytes 49156
  0.1 46.9 %copy-start.2 = (s32[8]{0:T(128)S(1)}, s32[8]{0:T(128)}, u32[]{:S(2)}) copy-start(s32[8]{0:T(128)} %refs_0_.3) | copy-start | bytes 100
  0.1 46.9 %copy-start.3 = (f32[128]{0:T(128)S(1)}, f32[128]{0:T(128)}, u32[]{:S(2)}) copy-start(f32[128]{0:T(128)} %param.21) | copy-start | bytes 1540
  0.1 46.9 %copy-start.1 = (f32[1,4096]{1,0:T(1,128)S(1)}, f32[1,4096]{1,0:T(1,128)}, u32[]{:S(2)}) copy-start(f32[1,4096]{1,0:T(1,128)} %param.20) | copy-start | bytes 49156
  0.1 16.2 %copy-start.15 = (s32[2,2,2048]{2,1,0:T(2,128)S(1)}, s32[2,2,2048]{2,1,0:T(2,128)}, u32[]{:S(2)}) copy-start(s32[2,2,2048]{2,1,0:T(2,128)} %param.24) | copy-start | bytes 98308
  0.2 16.2 %copy-start.14 = (f32[2,2048]{1,0:T(2,128)S(1)}, f32[2,2048]{1,0:T(2,128)}, u32[]{:S(2)}) copy-start(f32[2,2048]{1,0:T(2,128)} %param.23) | copy-start | bytes 49156
  7.2 20.3 %all-to-all-start = ((f32[16,64,128]{2,1,0:T(8,128)}), f32[16,64,128]{2,1,0:T(8,128)S(1)}, u32[]{:S(2)}, u32[]{:S(2)}) async-start(f32[16,64,128]{2,1,0:T(8,128)} %forward.1), calls=%async_computation | async-start | bytes 1048576 | tf_op jit(solution)/shard_map/all_to_all | solution.py:500
  16.4 5.7 %collective-permute-start = (f32[4,16,128]{2,1,0:T(8,128)S(1)}, f32[4,16,128]{2,1,0:T(8,128)S(1)}, u32[]{:S(2)}, u32[]{:S(2)}) collective-permute-start(f32[4,16,128]{2,1,0:T(8,128)S(1)} %bitcast.16), channel_id=1, source_target_pairs={{0,0},{1,1},{2,2},{3,3},{4,4},{5,5},{6,6},{7,7},{9,8},{8,9},{11,10... | collective-permute-start | bytes 98312 | tf_op jit(solution)/shard_map/ppermute | solution.py:454
  22.0 1.2 %collective-permute-start.1 = (f32[4,16,128]{2,1,0:T(8,128)S(1)}, f32[4,16,128]{2,1,0:T(8,128)S(1)}, u32[]{:S(2)}, u32[]{:S(2)}) collective-permute-start(f32[4,16,128]{2,1,0:T(8,128)S(1)} %collective-permute-done.own), channel_id=1, source_target_pairs={{0,8},{8,0},{16,24},{24,16},{32,40},{40,32},{48,56},{56,48},{64,72... | collective-permute-start | bytes 98312 | tf_op jit(solution)/shard_map/ppermute | solution.py:455

commit v3 on v2

--- a/solution.py
+++ b/solution.py
@@ -81,10 +81,6 @@
     return out_re, out_im
 
 
-def dot_nt(a, b):
-    return lax.dot_general(a, b, (((1,), (1,)), ((), ())), preferred_element_type=F32)
-
-
 def dot_nn(a, b):
     return lax.dot_general(a, b, (((1,), (0,)), ((), ())), preferred_element_type=F32)
 
@@ -92,37 +88,19 @@
 def product(x, table_hi, table_lo):
     high, low = split(x)
     return dot_nn(high, table_hi) + dot_nn(low, table_hi) + dot_nn(high, table_lo)
-
-
-def turned_rows(re, im, half):
-    left, right = [], []
-    for at in range(0, re.shape[0], half):
-        a, b = re[at : at + half], im[at : at + half]
-        left += [a, b]
-        right += [b, -a]
-    return jnp.concatenate([jnp.concatenate(left, 0), jnp.concatenate(right, 0)], 1)
-
-
-def turned_halves(pairs, half):
-    highs, lows = [], []
-    for re, im in pairs:
-        (rh, rl), (ih, il) = split(re), split(im)
-        highs.append(turned_rows(rh, ih, half))
-        lows.append(turned_rows(rl, il, half))
-    return jnp.concatenate(highs, 0), jnp.concatenate(lows, 0)
-
-
-def columns_product(table, table_hi, pairs, half):
-    high, low = turned_halves(pairs, half)
-    n = table_hi.shape[0]
-    both = dot_nt(table, high)
-    return both[:n] + both[n:] + dot_nt(table_hi, low)
 
 
 def side_by_side(x, half):
     re = [x[at : at + half] for at in range(0, x.shape[0], 2 * half)]
     im = [x[at + half : at + 2 * half] for at in range(0, x.shape[0], 2 * half)]
     return jnp.concatenate([jnp.concatenate(re, 0), jnp.concatenate(im, 0)], 1)
+
+
+def one_below_other(x, half):
+    parts = []
+    for at in range(0, x.shape[0], half):
+        parts += [x[at : at + half, :LANES], x[at : at + half, LANES:]]
+    return jnp.concatenate(parts, 0)
 
 
 PITCH = LANES + 16
@@ -149,8 +127,8 @@
 
 
 def forward_kernel(
-    subs, pairs, per_owner, offsets, facets, corr_h, tw_h, line_h, block_h, window_h, out, xr, xi, yr, yi, spec, corr, tw, line,
-    block, window, sems, table_sems
+    subs, pairs, per_owner, offsets, facets, corr_h, tw_h, line_h, block_h, window_h, out_h, xr, xi, yr, yi, spec, corr, tw, line,
+    block, window, out, sems, table_sems, out_sems
 ):
     rows = xr.shape[0]
     outer = yr.shape[0]
@@ -198,21 +176,23 @@
     for c in tables[2:]:
         c.wait()
 
-    def second(j, carry):
-        z = columns_product(line[...], line[:LANES, :], [(yr[2 * j + e], yi[2 * j + e]) for e in range(2)], half)
-        for e in range(2):
-            at = pl.multiple_of((2 * j + e) * PITCH + FRONT, 8)
-            spec[pl.ds(at, LANES), :] = z[:, e * LANES : (e + 1) * LANES]
-            spec[pl.ds(at + LANES, 8), :] = z[0:8, e * LANES : (e + 1) * LANES]
-        return carry
-
-    lax.fori_loop(0, outer // 2, second, 0, unroll=2)
+    per_step = 8
+    for j in range(outer // per_step):
+        ks = range(j * per_step, (j + 1) * per_step)
+        left = jnp.concatenate([yr[k] for k in ks], 0)
+        right = jnp.concatenate([yi[k] for k in ks], 0)
+        p = product(jnp.concatenate([left, right], 1), line[0], line[1])
+        for e, k in enumerate(ks):
+            z = one_below_other(p[e * rows : (e + 1) * rows], half).T
+            spec[k * PITCH + FRONT : k * PITCH + FRONT + LANES, :] = z
+            spec[k * PITCH + FRONT + LANES : k * PITCH + FRONT + LANES + 8, :] = z[0:8]
     top = block[...] * window_column(window[...], outer)
     bottom = jnp.concatenate([-top[:, LANES:], top[:, :LANES]], 1)
     table_hi, table_lo = split(jnp.concatenate([top, bottom], 0))
     near = lax.broadcasted_iota(jnp.int32, (8, LANES), 0) < 4
     slots = out.shape[0] // 2
-    batch = 4
+    batch = 2
+    sends = []
     for first_slot in range(0, slots, batch):
         stacked = []
         for slot in range(first_slot, first_slot + batch):
@@ -229,6 +209,11 @@
                 at = (2 * e + h) * half
                 out[2 * (first_slot + e) + h, 0:half, :] = p[at : at + half, :LANES]
                 out[2 * (first_slot + e) + h, half : 2 * half, :] = p[at : at + half, LANES:]
+        blocks = pl.ds(2 * first_slot, 2 * batch)
+        sends.append(pltpu.make_async_copy(out.at[blocks], out_h.at[blocks], out_sems.at[first_slot // batch]))
+        sends[-1].start()
+    for c in sends:
+        c.wait()
 
 
 def ready_kernel(own, other, out):
@@ -330,22 +315,24 @@
     half = rows // 2
     groups = rows // 8
     acc[...] = jnp.zeros(acc.shape, F32)
-    table_hi, table_lo = split(block[...] * window_column(window[...], outer))
-    table = jnp.concatenate([table_hi, table_lo], 0)
+    scale = jnp.broadcast_to(window_column(window[...], outer), (LANES, LANES)).T
+    cos, sin = block[:, :LANES] * scale, block[:, LANES:] * scale
+    top, bottom = jnp.concatenate([cos, -sin], 1), jnp.concatenate([sin, cos], 1)
+    table_hi, table_lo = split(jnp.concatenate([top, bottom], 0))
     near = lax.broadcasted_iota(jnp.int32, (8, LANES), 0) < 4
     slots = x.shape[0] // 2
-    for first_slot in range(0, slots, 2):
-        parts = []
-        for slot in range(first_slot, first_slot + 2):
-            re = jnp.concatenate([x[2 * slot, 0:half, :], x[2 * slot + 1, 0:half, :]], 0)
-            im = jnp.concatenate([x[2 * slot, half : 2 * half, :], x[2 * slot + 1, half : 2 * half, :]], 0)
-            parts.append((re, im))
-        z = columns_product(table, table_hi, parts, half)
-        for e in range(2):
+    group = 4
+    for first_slot in range(0, slots, group):
+        blocks = range(2 * first_slot, 2 * (first_slot + group))
+        re = jnp.concatenate([x[d, 0:half, :] for d in blocks], 0)
+        im = jnp.concatenate([x[d, half : 2 * half, :] for d in blocks], 0)
+        p = product(jnp.concatenate([re, im], 1), table_hi, table_lo)
+        for e in range(group):
+            z = one_below_other(p[e * rows : (e + 1) * rows], half).T
             offset = slot_offset(offsets, first_slot + e, subs, per_owner)
             at, value = [], []
             for c in range(outer):
-                block_rows = z[(c // 2) * 8 : (c // 2) * 8 + 8, e * LANES : (e + 1) * LANES]
+                block_rows = z[(c // 2) * 8 : (c // 2) * 8 + 8]
                 at.append(pl.ds(piece_row(offset, c, outer) - (c % 2) * 4, 8))
                 keep = near if c % 2 == 0 else jnp.logical_not(near)
                 value.append(acc[at[c], :] + jnp.where(keep, block_rows, 0.0))
@@ -370,7 +357,7 @@
             yi[k] = re * s + im * c
         return carry
 
-    lax.fori_loop(0, outer // batch, second, 0)
+    lax.fori_loop(0, outer // batch, second, 0, unroll=outer // batch)
 
     def copies(g):
         at = pl.ds(g * 8, 8)
@@ -468,16 +455,17 @@
     tw_both = jnp.asarray(np.concatenate(tw, 0), F32)
     c128, s128 = trig(LANES, LANES, LANES)
     corr = correction.reshape(outer, LANES)
-    line = jnp.asarray(np.concatenate(np_halves(np.concatenate([c128, s128], 1) * length**-0.5), 0))
+    line = jnp.asarray(np.stack(np_halves(np.block([[c128, -s128], [s128, c128]]) * length**-0.5)))
     per = LANES // outer
     order = np.array([m // per + outer * (m % per) for m in range(LANES)])
     block = jnp.asarray(np.concatenate([c128[order], s128[order]], 1) * LANES**-0.5, F32)
+    back_block = jnp.asarray(np.concatenate([c128[:, order], s128[:, order]], 1) * LANES**-0.5, F32)
     window = window.reshape(1, LANES)
 
     sent = pl.pallas_call(
         lambda *refs: forward_kernel(sub_count, pair_count, per_owner, *refs),
         in_specs=[smem()] + [hbm()] * 6,
-        out_specs=vmem(),
+        out_specs=hbm(),
         scratch_shapes=[
             pltpu.VMEM((rows, length), F32),
             pltpu.VMEM((rows, length), F32),
@@ -489,8 +477,10 @@
             pltpu.VMEM(line.shape, BF16),
             pltpu.VMEM(block.shape, F32),
             pltpu.VMEM(window.shape, F32),
+            pltpu.VMEM((facet_count, rows, LANES), F32),
             pltpu.SemaphoreType.DMA((2, rows // 8)),
             pltpu.SemaphoreType.DMA((5,)),
+            pltpu.SemaphoreType.DMA((facet_count // 4,)),
         ],
         out_shape=jax.ShapeDtypeStruct((facet_count, rows, LANES), F32),
         compiler_params=params(60),
@@ -532,7 +522,7 @@
         compiler_params=params(16),
         cost_estimate=cost(10**9, 10**7),
         name="backward",
-    )(offsets, back, corr, tw_cos, tw_sin, block, window, line_hi, line_lo)
+    )(offsets, back, corr, tw_cos, tw_sin, back_block, window, line_hi, line_lo)
     return result.reshape(1, rows, 2, length)
 
 

time: 53.4 us -> 50.5 us (0.946)
  Pallas kernels: 16.7 us -> 13.8 us
    pallas_call x1, Pallas kernels: 6.11 us -> 4.53 us  [on_device(): pl.pallas_call(lambda *refs: backward_kernel(sub_count, per_owner, *refs)...]
    pallas_call x1, Pallas kernels: 7.02 us -> 5.66 us  [on_device(): pl.pallas_call(lambda *refs: forward_kernel(sub_count, pair_count, per_ow...]
where the time goes in v3:
time: 50.5 us; the launch traced here: 50.2 us
  blocking collectives  16.2 us (32%)
  Pallas kernels  13.8 us (27%)
  starting transfers between devices  11.8 us (23%)
  waiting for transfers between devices  8.07 us (16%)
    all_to_all x1, blocking collectives, on_device(): lax.all_to_all(adjoint, 'facet', split_axis=0, concat_axis=0, tiled=True)  16.2 us
    all_to_all x1, starting transfers between devices, on_device(): got = lax.all_to_all(sent, 'facet', split_axis=0, concat_axis=0, tiled=True)  9.13 us
    pallas_call x1, Pallas kernels, on_device(): pl.pallas_call(lambda *refs: forward_kernel(sub_count, pair_count, per_ow...  5.66 us
    pallas_call x1, Pallas kernels, on_device(): pl.pallas_call(lambda *refs: backward_kernel(sub_count, per_owner, *refs)...  4.53 us
    all_to_all x1, waiting for transfers between devices, on_device(): got = lax.all_to_all(sent, 'facet', split_axis=0, concat_axis=0, tiled=True)  3.86 us
    pallas_call x1, Pallas kernels, on_device(): pl.pallas_call(middle_kernel, in_specs=[vmem()] * 8, out_specs=vmem(), sc...  3.19 us
    ppermute x1, waiting for transfers between devices, on_device(): fetched = lax.ppermute(payload, names, route)  3 us
    ppermute x1, starting transfers between devices, on_device(): fetched = lax.ppermute(payload, names, route)  2.64 us
  transfers between devices with their start and end apart: 3, of which 3 were waited for; matrix products, arithmetic and copies ran while one was open for 0% of the time, Pallas kernels for 1%

profile of v3, /device:TPU:1, one launch (start us, length us, event | category | flops | bytes accessed | tf_op | source)
XLA Modules:
  0.0 50.2 jit_solution(2185297063356179721)
XLA Ops:
  0.0 0.0 copy-start.12
  0.0 0.0 copy-start.13
  0.0 0.0 copy-start.6
  0.0 0.0 copy-start.7
  0.0 0.0 copy-start.8
  0.0 0.0 copy-start.9
  0.0 0.0 copy-start.3
  0.1 0.0 copy-start.4
  0.1 0.0 copy-start.5
  0.1 0.0 copy-start.10
  0.1 0.0 copy-start.11
  0.1 0.0 copy-start.1
  0.1 0.0 copy-start.2
  0.1 0.0 copy-start
  0.1 0.0 copy-start.15
  0.2 0.0 copy-start.14
  0.2 5.7 %forward.1 = f32[16,64,128]{2,1,0:T(8,128)} custom-call(s32[8]{0:T(128)} %refs_0_.3, f32[512,2,4096]{2,1,0:T(2,128)} %bitcast.15, f32[32,128]{1,0:T(8,128)} %bitcast.11, f32[64,128]{1,0:T(8,128)} %constant.64.clone.refs_3_, bf16[2,256,256]{2,1,0:T(8,128)(2,1)} %constant.65.clone.refs_4_, f32[128,256]{1,0:T(8,128)} %constant.66.clone.refs_5_, f32[1,128]{1,0:T(1,128)} %bitcast.13), custom_call_target="tpu_custom_call" | custom-call | flops 1000000000 | bytes 10000000 | tf_op jit(solution)/shard_map/forward/pallas_call | solution.py:465
  5.8 9.1 %all-to-all-start = ((f32[16,64,128]{2,1,0:T(8,128)}), f32[16,64,128]{2,1,0:T(8,128)S(1)}, u32[]{:S(2)}, u32[]{:S(2)}) async-start(f32[16,64,128]{2,1,0:T(8,128)} %forward.1), calls=%async_computation | async-start | bytes 1048576 | tf_op jit(solution)/shard_map/all_to_all | solution.py:490
  15.0 0.0 copy-done.15
  15.0 0.0 copy-done.14
  15.0 2.6 %collective-permute-start = (f32[4,16,128]{2,1,0:T(8,128)S(1)}, f32[4,16,128]{2,1,0:T(8,128)S(1)}, u32[]{:S(2)}, u32[]{:S(2)}) collective-permute-start(f32[4,16,128]{2,1,0:T(8,128)S(1)} %bitcast.16), channel_id=1, source_target_pairs={{0,0},{1,1},{2,2},{3,3},{4,4},{5,5},{6,6},{7,7},{9,8},{8,9},{11,10... | collective-permute-start | bytes 98312 | tf_op jit(solution)/shard_map/ppermute | solution.py:441
  17.7 3.0 %collective-permute-done.own = f32[4,16,128]{2,1,0:T(8,128)S(1)} collective-permute-done((f32[4,16,128]{2,1,0:T(8,128)S(1)}, f32[4,16,128]{2,1,0:T(8,128)S(1)}, u32[]{:S(2)}, u32[]{:S(2)}) %collective-permute-start) | collective-permute-done | bytes 32800 | tf_op jit(solution)/shard_map/ppermute | solution.py:441
  20.7 0.0 collective-permute-start.1
  20.7 1.2 %collective-permute-done.1.other = f32[4,16,128]{2,1,0:T(8,128)S(1)} collective-permute-done((f32[4,16,128]{2,1,0:T(8,128)S(1)}, f32[4,16,128]{2,1,0:T(8,128)S(1)}, u32[]{:S(2)}, u32[]{:S(2)}) %collective-permute-start.1) | collective-permute-done | bytes 32800 | tf_op jit(solution)/shard_map/ppermute | solution.py:442
  21.9 0.4 ready.1
  22.3 3.9 %all-to-all-done.x = f32[16,64,128]{2,1,0:T(8,128)S(1)} async-done(((f32[16,64,128]{2,1,0:T(8,128)}), f32[16,64,128]{2,1,0:T(8,128)S(1)}, u32[]{:S(2)}, u32[]{:S(2)}) %all-to-all-start) | async-done | bytes 524320 | tf_op jit(solution)/shard_map/all_to_all | solution.py:490
  26.2 0.0 copy-done.12
  26.2 0.0 copy-done.13
  26.2 0.0 copy-done.6
  26.2 0.0 copy-done.7
  26.2 0.0 copy-done.8
  26.2 0.0 copy-done.9
  26.2 3.2 %middle.1 = f32[16,64,128]{2,1,0:T(8,128)S(1)} custom-call(f32[16,64,128]{2,1,0:T(8,128)S(1)} %all-to-all-done.x, f32[3,4,16,128]{3,2,1,0:T(8,128)S(1)} %ready.1, f32[16,128]{1,0:T(8,128)S(1)} %copy-done.13, f32[16,128]{1,0:T(8,128)S(1)} %copy-done.12, bf16[256,256]{1,0:T(8,128)(2,1)S(1)} %copy-done.9, bf16[256,256]{1,0:T(8,128)(2,1)S(1)} %copy-done.8, ...), custom_call_target="tpu_custom_call" | custom-call | flops 1000000000 | bytes 10000000 | tf_op jit(solution)/shard_map/middle/pallas_call | solution.py:496
  29.4 16.2 %all_to_all.10.refs_1_ = f32[16,64,128]{2,1,0:T(8,128)S(1)} all-to-all(f32[16,64,128]{2,1,0:T(8,128)S(1)} %middle.1), channel_id=1, replica_groups=mesh['facet'=16,'sub'=4,'wa'=2] {'facet'}, dimensions={0} | all-to-all | bytes 1048576 | tf_op jit(solution)/shard_map/all_to_all | solution.py:506
  45.6 0.0 copy-done.3
  45.6 0.0 copy-done.4
  45.6 0.0 copy-done.5
  45.6 0.0 copy-done.10
  45.6 0.0 copy-done.11
  45.6 0.0 copy-done.1
  45.6 0.0 copy-done.2
  45.6 0.0 copy-done
  45.6 4.5 %backward.1 = f32[64,2,4096]{2,1,0:T(2,128)} custom-call(s32[8]{0:T(128)S(1)} %copy-done.1, f32[16,64,128]{2,1,0:T(8,128)S(1)} %all_to_all.10.refs_1_, f32[32,128]{1,0:T(8,128)S(1)} %bitcast.12, f32[32,128]{1,0:T(8,128)S(1)} %copy-done.11, f32[32,128]{1,0:T(8,128)S(1)} %copy-done.10, f32[128,256]{1,0:T(8,128)S(1)} %copy-done.5, f32[1,128]{1,0:T(1,128)S(1)} %bitcast.14, ...), custom_call_target="tpu_custom_call" | custom-call | flops 1000000000 | bytes 10000000 | tf_op jit(solution)/shard_map/backward/pallas_call | solution.py:509
  (3 shorter events, 0.0 us)
Async XLA Ops:
  0.0 26.2 %copy-start.12 = (f32[16,128]{1,0:T(8,128)S(1)}, f32[16,128]{1,0:T(8,128)}, u32[]{:S(2)}) copy-start(f32[16,128]{1,0:T(8,128)} %constant.73.clone.tw_sin) | copy-start | bytes 24580
  0.0 26.2 %copy-start.13 = (f32[16,128]{1,0:T(8,128)S(1)}, f32[16,128]{1,0:T(8,128)}, u32[]{:S(2)}) copy-start(f32[16,128]{1,0:T(8,128)} %constant.72.clone.tw_cos) | copy-start | bytes 24580
  0.0 26.2 %copy-start.6 = (bf16[256,256]{1,0:T(8,128)(2,1)S(1)}, bf16[256,256]{1,0:T(8,128)(2,1)}, u32[]{:S(2)}) copy-start(bf16[256,256]{1,0:T(8,128)(2,1)} %constant.71.clone.bwd_lo) | copy-start | bytes 393220
  0.0 26.2 %copy-start.7 = (bf16[256,256]{1,0:T(8,128)(2,1)S(1)}, bf16[256,256]{1,0:T(8,128)(2,1)}, u32[]{:S(2)}) copy-start(bf16[256,256]{1,0:T(8,128)(2,1)} %constant.70.clone.bwd_hi) | copy-start | bytes 393220
  0.0 26.2 %copy-start.8 = (bf16[256,256]{1,0:T(8,128)(2,1)S(1)}, bf16[256,256]{1,0:T(8,128)(2,1)}, u32[]{:S(2)}) copy-start(bf16[256,256]{1,0:T(8,128)(2,1)} %constant.69.clone.fwd_lo) | copy-start | bytes 393220
  0.0 26.2 %copy-start.9 = (bf16[256,256]{1,0:T(8,128)(2,1)S(1)}, bf16[256,256]{1,0:T(8,128)(2,1)}, u32[]{:S(2)}) copy-start(bf16[256,256]{1,0:T(8,128)(2,1)} %constant.68.clone.fwd_hi) | copy-start | bytes 393220
  0.0 45.5 %copy-start.3 = (bf16[256,256]{1,0:T(8,128)(2,1)S(1)}, bf16[256,256]{1,0:T(8,128)(2,1)}, u32[]{:S(2)}) copy-start(bf16[256,256]{1,0:T(8,128)(2,1)} %constant.75.clone.refs_8_) | copy-start | bytes 393220
  0.1 45.5 %copy-start.4 = (bf16[256,256]{1,0:T(8,128)(2,1)S(1)}, bf16[256,256]{1,0:T(8,128)(2,1)}, u32[]{:S(2)}) copy-start(bf16[256,256]{1,0:T(8,128)(2,1)} %constant.74.clone.refs_7_) | copy-start | bytes 393220
  0.1 45.5 %copy-start.5 = (f32[128,256]{1,0:T(8,128)S(1)}, f32[128,256]{1,0:T(8,128)}, u32[]{:S(2)}) copy-start(f32[128,256]{1,0:T(8,128)} %constant.67.clone.refs_5_) | copy-start | bytes 393220
  0.1 45.5 %copy-start.10 = (f32[32,128]{1,0:T(8,128)S(1)}, f32[32,128]{1,0:T(8,128)}, u32[]{:S(2)}) copy-start(f32[32,128]{1,0:T(8,128)} %constant.63.clone.refs_4_) | copy-start | bytes 49156
  0.1 45.5 %copy-start.11 = (f32[32,128]{1,0:T(8,128)S(1)}, f32[32,128]{1,0:T(8,128)}, u32[]{:S(2)}) copy-start(f32[32,128]{1,0:T(8,128)} %constant.62.clone.refs_3_) | copy-start | bytes 49156
  0.1 45.5 %copy-start.1 = (s32[8]{0:T(128)S(1)}, s32[8]{0:T(128)}, u32[]{:S(2)}) copy-start(s32[8]{0:T(128)} %refs_0_.3) | copy-start | bytes 100
  0.1 45.5 %copy-start.2 = (f32[128]{0:T(128)S(1)}, f32[128]{0:T(128)}, u32[]{:S(2)}) copy-start(f32[128]{0:T(128)} %param.22) | copy-start | bytes 1540
  0.1 45.5 %copy-start = (f32[1,4096]{1,0:T(1,128)S(1)}, f32[1,4096]{1,0:T(1,128)}, u32[]{:S(2)}) copy-start(f32[1,4096]{1,0:T(1,128)} %param.21) | copy-start | bytes 49156
  0.1 14.8 %copy-start.15 = (s32[2,2,2048]{2,1,0:T(2,128)S(1)}, s32[2,2,2048]{2,1,0:T(2,128)}, u32[]{:S(2)}) copy-start(s32[2,2,2048]{2,1,0:T(2,128)} %param.25) | copy-start | bytes 98308
  0.2 14.8 %copy-start.14 = (f32[2,2048]{1,0:T(2,128)S(1)}, f32[2,2048]{1,0:T(2,128)}, u32[]{:S(2)}) copy-start(f32[2,2048]{1,0:T(2,128)} %param.24) | copy-start | bytes 49156
  5.8 20.3 %all-to-all-start = ((f32[16,64,128]{2,1,0:T(8,128)}), f32[16,64,128]{2,1,0:T(8,128)S(1)}, u32[]{:S(2)}, u32[]{:S(2)}) async-start(f32[16,64,128]{2,1,0:T(8,128)} %forward.1), calls=%async_computation | async-start | bytes 1048576 | tf_op jit(solution)/shard_map/all_to_all | solution.py:490
  15.0 5.7 %collective-permute-start = (f32[4,16,128]{2,1,0:T(8,128)S(1)}, f32[4,16,128]{2,1,0:T(8,128)S(1)}, u32[]{:S(2)}, u32[]{:S(2)}) collective-permute-start(f32[4,16,128]{2,1,0:T(8,128)S(1)} %bitcast.16), channel_id=1, source_target_pairs={{0,0},{1,1},{2,2},{3,3},{4,4},{5,5},{6,6},{7,7},{9,8},{8,9},{11,10... | collective-permute-start | bytes 98312 | tf_op jit(solution)/shard_map/ppermute | solution.py:441
  20.7 1.2 %collective-permute-start.1 = (f32[4,16,128]{2,1,0:T(8,128)S(1)}, f32[4,16,128]{2,1,0:T(8,128)S(1)}, u32[]{:S(2)}, u32[]{:S(2)}) collective-permute-start(f32[4,16,128]{2,1,0:T(8,128)S(1)} %collective-permute-done.own), channel_id=1, source_target_pairs={{0,8},{8,0},{16,24},{24,16},{32,40},{40,32},{48,56},{56,48},{64,72... | collective-permute-start | bytes 98312 | tf_op jit(solution)/shard_map/ppermute | solution.py:442

commit v4 on v3

--- a/solution.py
+++ b/solution.py
@@ -127,7 +127,7 @@
 
 
 def forward_kernel(
-    subs, pairs, per_owner, offsets, facets, corr_h, tw_h, line_h, block_h, window_h, out_h, xr, xi, yr, yi, spec, corr, tw, line,
+    subs, pairs, per_owner, place, offsets, facets, corr_h, tw_h, line_h, block_h, window_h, out_h, xr, xi, yr, yi, spec, corr, tw, line,
     block, window, out, sems, table_sems, out_sems
 ):
     rows = xr.shape[0]
@@ -207,11 +207,11 @@
         for e in range(batch):
             for h in range(2):
                 at = (2 * e + h) * half
-                out[2 * (first_slot + e) + h, 0:half, :] = p[at : at + half, :LANES]
-                out[2 * (first_slot + e) + h, half : 2 * half, :] = p[at : at + half, LANES:]
-        blocks = pl.ds(2 * first_slot, 2 * batch)
-        sends.append(pltpu.make_async_copy(out.at[blocks], out_h.at[blocks], out_sems.at[first_slot // batch]))
-        sends[-1].start()
+                to = place[2 * (first_slot + e) + h]
+                out[to, 0:half, :] = p[at : at + half, :LANES]
+                out[to, half : 2 * half, :] = p[at : at + half, LANES:]
+                sends.append(pltpu.make_async_copy(out.at[to], out_h.at[to], out_sems.at[to]))
+                sends[-1].start()
     for c in sends:
         c.wait()
 
@@ -234,7 +234,7 @@
             out[1, at + w] = jnp.sin(src[planes + w])
 
 
-def middle_kernel(x, ready, tw_cos, tw_sin, fwd_hi, fwd_lo, bwd_hi, bwd_lo, out, br, bi, qr, qi):
+def middle_kernel(place, x, ready, tw_cos, tw_sin, fwd_hi, fwd_lo, bwd_hi, bwd_lo, out, br, bi, qr, qi):
     outer = x.shape[0]
     rows = x.shape[1] // 2
     groups = rows // 8
@@ -247,7 +247,7 @@
         re, im = [], []
         for a in range(outer):
             c, s = ready[0, w, a : a + 1, :], ready[1, w, a : a + 1, :]
-            p, q = x[a, top, :], x[a, bot, :]
+            p, q = x[place[a], top, :], x[place[a], bot, :]
             re.append(p * c - q * s)
             im.append(p * s + q * c)
         re, im = small_fft(re, im, -1.0)
@@ -264,12 +264,13 @@
         for a in range(outer):
             c, s = ready[0, w, a : a + 1, :], ready[1, w, a : a + 1, :]
             hr, hi = re[a] * c + im[a] * s, im[a] * c - re[a] * s
+            to = place[a]
             if w == 0:
-                out[a, top, :] = hr
-                out[a, bot, :] = hi
+                out[to, top, :] = hr
+                out[to, bot, :] = hi
             else:
-                out[a, top, :] += hr
-                out[a, bot, :] += hi
+                out[to, top, :] += hr
+                out[to, bot, :] += hi
 
     def to_grid(w, part):
         at = range(part * step, (part + 1) * step)
@@ -308,7 +309,7 @@
 
 
 def backward_kernel(
-    subs, per_owner, offsets, x, corr, tw_cos, tw_sin, block, window, line_hi, line_lo, out, acc, yr, yi, zr, zi, sems
+    subs, per_owner, place, offsets, x, corr, tw_cos, tw_sin, block, window, line_hi, line_lo, out, acc, yr, yi, zr, zi, sems
 ):
     rows = zr.shape[0]
     outer = yr.shape[0]
@@ -323,7 +324,7 @@
     slots = x.shape[0] // 2
     group = 4
     for first_slot in range(0, slots, group):
-        blocks = range(2 * first_slot, 2 * (first_slot + group))
+        blocks = [place[d] for d in range(2 * first_slot, 2 * (first_slot + group))]
         re = jnp.concatenate([x[d, 0:half, :] for d in blocks], 0)
         im = jnp.concatenate([x[d, half : 2 * half, :] for d in blocks], 0)
         p = product(jnp.concatenate([re, im], 1), table_hi, table_lo)
@@ -411,6 +412,10 @@
     return pl.CostEstimate(flops=flops, bytes_accessed=nbytes, transcendentals=0)
 
 
+def exchange_order(count):
+    return list(range(count - 1, -1, -1))
+
+
 def on_device(facets, correction, window, offsets, phases, coverage):
     sub_count = lax.axis_size("sub")
     pair_count = lax.axis_size("wa")
@@ -422,6 +427,12 @@
     half = rows // 2
     per_owner = coverage.shape[0]
     width = facet_count * LANES
+
+    members = exchange_order(facet_count)
+    place = [members.index(f) for f in range(facet_count)]
+
+    def exchange(blocks):
+        return lax.all_to_all(blocks, "facet", split_axis=0, concat_axis=0, tiled=True, axis_index_groups=[members])
 
 
     slot = facet // 2
@@ -463,7 +474,7 @@
     window = window.reshape(1, LANES)
 
     sent = pl.pallas_call(
-        lambda *refs: forward_kernel(sub_count, pair_count, per_owner, *refs),
+        lambda *refs: forward_kernel(sub_count, pair_count, per_owner, place, *refs),
         in_specs=[smem()] + [hbm()] * 6,
         out_specs=hbm(),
         scratch_shapes=[
@@ -480,21 +491,21 @@
             pltpu.VMEM((facet_count, rows, LANES), F32),
             pltpu.SemaphoreType.DMA((2, rows // 8)),
             pltpu.SemaphoreType.DMA((5,)),
-            pltpu.SemaphoreType.DMA((facet_count // 4,)),
+            pltpu.SemaphoreType.DMA((facet_count,)),
         ],
         out_shape=jax.ShapeDtypeStruct((facet_count, rows, LANES), F32),
         compiler_params=params(60),
         cost_estimate=cost(10**9, 10**7),
         name="forward",
     )(offsets, facets.reshape(facets.shape[1:]), corr, tw_both, line, block, window)
-    got = lax.all_to_all(sent, "facet", split_axis=0, concat_axis=0, tiled=True)
+    got = exchange(sent)
 
     tw2 = trig(facet_count, LANES, width)
     fwd_hi, fwd_lo = halves(np.block([[c128, -s128], [s128, c128]]))
     inverse = np.block([[c128, s128], [-s128, c128]])
     bwd_hi, bwd_lo = halves(inverse * (1.0 / (width * WPLANES)))
     adjoint = pl.pallas_call(
-        middle_kernel,
+        lambda *refs: middle_kernel(place, *refs),
         in_specs=[vmem()] * 8,
         out_specs=vmem(),
         scratch_shapes=[pltpu.VMEM((2, facet_count, half, LANES), F32)] * 4,
@@ -503,11 +514,11 @@
         cost_estimate=cost(10**9, 10**7),
         name="middle",
     )(got, ready, jnp.asarray(tw2[0], F32), jnp.asarray(tw2[1], F32), fwd_hi, fwd_lo, bwd_hi, bwd_lo)
-    back = lax.all_to_all(adjoint, "facet", split_axis=0, concat_axis=0, tiled=True)
+    back = exchange(adjoint)
 
     line_hi, line_lo = halves(inverse * length**-0.5)
     result = pl.pallas_call(
-        lambda *refs: backward_kernel(sub_count, per_owner, *refs),
+        lambda *refs: backward_kernel(sub_count, per_owner, place, *refs),
         in_specs=[smem()] + [vmem()] * 8,
         out_specs=hbm(),
         scratch_shapes=[

time: 50.5 us -> 46.8 us (0.927)
  blocking collectives: 16.2 us -> 13.5 us
  waiting for transfers between devices: 8.07 us -> 6.03 us
  starting transfers between devices: 11.8 us -> 12.7 us
    all_to_all x1, waiting for transfers between devices: 3.86 us -> 0.01 us  [exchange(): lax.all_to_all(blocks, 'facet', split_axis=0, concat_axis=0, tiled=True,...]
    all_to_all x1, blocking collectives: 16.2 us -> 13.5 us  [exchange(): lax.all_to_all(blocks, 'facet', split_axis=0, concat_axis=0, tiled=True,...]
    ppermute x1, waiting for transfers between devices: 3 us -> 4.83 us  [on_device(): fetched = lax.ppermute(payload, names, route)]
    all_to_all x1, starting transfers between devices: 9.13 us -> 10.1 us  [exchange(): lax.all_to_all(blocks, 'facet', split_axis=0, concat_axis=0, tiled=True,...]
  transfers between devices with their start and end apart: 3 -> 3, of which waited for: 3 -> 2; matrix products, arithmetic and copies ran while one was open for 0% -> 0% of each run, Pallas kernels for 1% -> 1%
where the time goes in v4:
time: 46.8 us; the launch traced here: 46.5 us
  Pallas kernels  13.8 us (29%)
  blocking collectives  13.5 us (29%)
  starting transfers between devices  12.7 us (27%)
  waiting for transfers between devices  6.03 us (13%)
    all_to_all x1, blocking collectives, exchange(): lax.all_to_all(blocks, 'facet', split_axis=0, concat_axis=0, tiled=True,...  13.5 us
    all_to_all x1, starting transfers between devices, exchange(): lax.all_to_all(blocks, 'facet', split_axis=0, concat_axis=0, tiled=True,...  10.1 us
    pallas_call x1, Pallas kernels, on_device(): pl.pallas_call(lambda *refs: forward_kernel(sub_count, pair_count, per_ow...  5.73 us
    ppermute x1, waiting for transfers between devices, on_device(): fetched = lax.ppermute(payload, names, route)  4.83 us
    pallas_call x1, Pallas kernels, on_device(): pl.pallas_call(lambda *refs: backward_kernel(sub_count, per_owner, place,...  4.52 us
    pallas_call x1, Pallas kernels, on_device(): pl.pallas_call(lambda *refs: middle_kernel(place, *refs), in_specs=[vmem(...  3.19 us
    ppermute x1, starting transfers between devices, on_device(): fetched = lax.ppermute(payload, names, route)  2.65 us
    ppermute x1, waiting for transfers between devices, on_device(): lax.ppermute(fetched, 'facet', [(f, f ^ 1) for f in range(facet_count)])  1.2 us
  transfers between devices with their start and end apart: 3, of which 2 were waited for; matrix products, arithmetic and copies ran while one was open for 0% of the time, Pallas kernels for 1%

profile of v4, /device:TPU:1, one launch (start us, length us, event | category | flops | bytes accessed | tf_op | source)
XLA Modules:
  0.0 46.5 jit_solution(6325941795298394627)
XLA Ops:
  0.0 0.0 copy-start.12
  0.0 0.0 copy-start.13
  0.0 0.0 copy-start.6
  0.0 0.0 copy-start.7
  0.0 0.0 copy-start.8
  0.0 0.0 copy-start.9
  0.0 0.0 copy-start.3
  0.1 0.0 copy-start.4
  0.1 0.0 copy-start.5
  0.1 0.0 copy-start.10
  0.1 0.0 copy-start.11
  0.1 0.0 copy-start.1
  0.1 0.0 copy-start.2
  0.1 0.0 copy-start
  0.1 0.0 copy-start.15
  0.2 0.0 copy-start.14
  0.2 5.7 %forward.1 = f32[16,64,128]{2,1,0:T(8,128)} custom-call(s32[8]{0:T(128)} %refs_0_.3, f32[512,2,4096]{2,1,0:T(2,128)} %bitcast.15, f32[32,128]{1,0:T(8,128)} %bitcast.11, f32[64,128]{1,0:T(8,128)} %constant.64.clone.refs_3_, bf16[2,256,256]{2,1,0:T(8,128)(2,1)} %constant.65.clone.refs_4_, f32[128,256]{1,0:T(8,128)} %constant.66.clone.refs_5_, f32[1,128]{1,0:T(1,128)} %bitcast.13), custom_call_target="tpu_custom_call" | custom-call | flops 1000000000 | bytes 10000000 | tf_op jit(solution)/shard_map/forward/pallas_call | solution.py:476
  5.9 10.1 %all-to-all-start = ((f32[16,64,128]{2,1,0:T(8,128)}), f32[16,64,128]{2,1,0:T(8,128)S(1)}, u32[]{:S(2)}, u32[]{:S(2)}) async-start(f32[16,64,128]{2,1,0:T(8,128)} %forward.1), calls=%async_computation | async-start | bytes 1048576 | tf_op jit(solution)/shard_map/all_to_all | solution.py:435
  16.0 0.0 copy-done.15
  16.0 0.0 copy-done.14
  16.0 2.7 %collective-permute-start = (f32[4,16,128]{2,1,0:T(8,128)S(1)}, f32[4,16,128]{2,1,0:T(8,128)S(1)}, u32[]{:S(2)}, u32[]{:S(2)}) collective-permute-start(f32[4,16,128]{2,1,0:T(8,128)S(1)} %bitcast.16), channel_id=1, source_target_pairs={{0,0},{1,1},{2,2},{3,3},{4,4},{5,5},{6,6},{7,7},{9,8},{8,9},{11,10... | collective-permute-start | bytes 98312 | tf_op jit(solution)/shard_map/ppermute | solution.py:452
  18.7 4.8 %collective-permute-done.own = f32[4,16,128]{2,1,0:T(8,128)S(1)} collective-permute-done((f32[4,16,128]{2,1,0:T(8,128)S(1)}, f32[4,16,128]{2,1,0:T(8,128)S(1)}, u32[]{:S(2)}, u32[]{:S(2)}) %collective-permute-start) | collective-permute-done | bytes 32800 | tf_op jit(solution)/shard_map/ppermute | solution.py:452
  23.5 0.0 collective-permute-start.1
  23.5 1.2 %collective-permute-done.1.other = f32[4,16,128]{2,1,0:T(8,128)S(1)} collective-permute-done((f32[4,16,128]{2,1,0:T(8,128)S(1)}, f32[4,16,128]{2,1,0:T(8,128)S(1)}, u32[]{:S(2)}, u32[]{:S(2)}) %collective-permute-start.1) | collective-permute-done | bytes 32800 | tf_op jit(solution)/shard_map/ppermute | solution.py:453
  24.7 0.4 ready.1.refs_1_
  25.1 0.0 all-to-all-done.refs_0_
  25.1 0.0 copy-done.12
  25.1 0.0 copy-done.13
  25.2 0.0 copy-done.6
  25.2 0.0 copy-done.7
  25.2 0.0 copy-done.8
  25.2 0.0 copy-done.9
  25.2 3.2 %middle.1 = f32[16,64,128]{2,1,0:T(8,128)S(1)} custom-call(f32[16,64,128]{2,1,0:T(8,128)S(1)} %all-to-all-done.refs_0_, f32[3,4,16,128]{3,2,1,0:T(8,128)S(1)} %ready.1.refs_1_, f32[16,128]{1,0:T(8,128)S(1)} %copy-done.13, f32[16,128]{1,0:T(8,128)S(1)} %copy-done.12, bf16[256,256]{1,0:T(8,128)(2,1)S(1)} %copy-done.9, bf16[256,256]{1,0:T(8,128)(2,1)S(1)} %copy-done.8, ...), custom_call_target="tpu_custom_call" | custom-call | flops 1000000000 | bytes 10000000 | tf_op jit(solution)/shard_map/middle/pallas_call | solution.py:507
  28.4 13.5 %all_to_all.10.refs_1_ = f32[16,64,128]{2,1,0:T(8,128)S(1)} all-to-all(f32[16,64,128]{2,1,0:T(8,128)S(1)} %middle.1), channel_id=1, replica_groups={{120,112,104,96,88,80,72,64,56,48,40,32,24,16,8,0},{121,113,105,97,89,8..., dimensions={0} | all-to-all | bytes 1048576 | tf_op jit(solution)/shard_map/all_to_all | solution.py:435
  41.9 0.0 copy-done.3
  41.9 0.0 copy-done.4
  41.9 0.0 copy-done.5
  41.9 0.0 copy-done.10
  41.9 0.0 copy-done.11
  41.9 0.0 copy-done.1
  41.9 0.0 copy-done.2
  41.9 0.0 copy-done
  42.0 4.5 %backward.1 = f32[64,2,4096]{2,1,0:T(2,128)} custom-call(s32[8]{0:T(128)S(1)} %copy-done.1, f32[16,64,128]{2,1,0:T(8,128)S(1)} %all_to_all.10.refs_1_, f32[32,128]{1,0:T(8,128)S(1)} %bitcast.12, f32[32,128]{1,0:T(8,128)S(1)} %copy-done.11, f32[32,128]{1,0:T(8,128)S(1)} %copy-done.10, f32[128,256]{1,0:T(8,128)S(1)} %copy-done.5, f32[1,128]{1,0:T(1,128)S(1)} %bitcast.14, ...), custom_call_target="tpu_custom_call" | custom-call | flops 1000000000 | bytes 10000000 | tf_op jit(solution)/shard_map/backward/pallas_call | solution.py:520
  (3 shorter events, 0.0 us)
Async XLA Ops:
  0.0 25.1 %copy-start.12 = (f32[16,128]{1,0:T(8,128)S(1)}, f32[16,128]{1,0:T(8,128)}, u32[]{:S(2)}) copy-start(f32[16,128]{1,0:T(8,128)} %constant.73.clone.refs_3_) | copy-start | bytes 24580
  0.0 25.1 %copy-start.13 = (f32[16,128]{1,0:T(8,128)S(1)}, f32[16,128]{1,0:T(8,128)}, u32[]{:S(2)}) copy-start(f32[16,128]{1,0:T(8,128)} %constant.72.clone.refs_2_) | copy-start | bytes 24580
  0.0 25.2 %copy-start.6 = (bf16[256,256]{1,0:T(8,128)(2,1)S(1)}, bf16[256,256]{1,0:T(8,128)(2,1)}, u32[]{:S(2)}) copy-start(bf16[256,256]{1,0:T(8,128)(2,1)} %constant.71.clone.refs_7_) | copy-start | bytes 393220
  0.0 25.2 %copy-start.7 = (bf16[256,256]{1,0:T(8,128)(2,1)S(1)}, bf16[256,256]{1,0:T(8,128)(2,1)}, u32[]{:S(2)}) copy-start(bf16[256,256]{1,0:T(8,128)(2,1)} %constant.70.clone.refs_6_) | copy-start | bytes 393220
  0.0 25.2 %copy-start.8 = (bf16[256,256]{1,0:T(8,128)(2,1)S(1)}, bf16[256,256]{1,0:T(8,128)(2,1)}, u32[]{:S(2)}) copy-start(bf16[256,256]{1,0:T(8,128)(2,1)} %constant.69.clone.refs_5_) | copy-start | bytes 393220
  0.0 25.2 %copy-start.9 = (bf16[256,256]{1,0:T(8,128)(2,1)S(1)}, bf16[256,256]{1,0:T(8,128)(2,1)}, u32[]{:S(2)}) copy-start(bf16[256,256]{1,0:T(8,128)(2,1)} %constant.68.clone.refs_4_) | copy-start | bytes 393220
  0.0 41.8 %copy-start.3 = (bf16[256,256]{1,0:T(8,128)(2,1)S(1)}, bf16[256,256]{1,0:T(8,128)(2,1)}, u32[]{:S(2)}) copy-start(bf16[256,256]{1,0:T(8,128)(2,1)} %constant.75.clone.refs_8_) | copy-start | bytes 393220
  0.1 41.8 %copy-start.4 = (bf16[256,256]{1,0:T(8,128)(2,1)S(1)}, bf16[256,256]{1,0:T(8,128)(2,1)}, u32[]{:S(2)}) copy-start(bf16[256,256]{1,0:T(8,128)(2,1)} %constant.74.clone.refs_7_) | copy-start | bytes 393220
  0.1 41.8 %copy-start.5 = (f32[128,256]{1,0:T(8,128)S(1)}, f32[128,256]{1,0:T(8,128)}, u32[]{:S(2)}) copy-start(f32[128,256]{1,0:T(8,128)} %constant.67.clone.refs_5_) | copy-start | bytes 393220
  0.1 41.8 %copy-start.10 = (f32[32,128]{1,0:T(8,128)S(1)}, f32[32,128]{1,0:T(8,128)}, u32[]{:S(2)}) copy-start(f32[32,128]{1,0:T(8,128)} %constant.63.clone.refs_4_) | copy-start | bytes 49156
  0.1 41.8 %copy-start.11 = (f32[32,128]{1,0:T(8,128)S(1)}, f32[32,128]{1,0:T(8,128)}, u32[]{:S(2)}) copy-start(f32[32,128]{1,0:T(8,128)} %constant.62.clone.refs_3_) | copy-start | bytes 49156
  0.1 41.8 %copy-start.1 = (s32[8]{0:T(128)S(1)}, s32[8]{0:T(128)}, u32[]{:S(2)}) copy-start(s32[8]{0:T(128)} %refs_0_.3) | copy-start | bytes 100
  0.1 41.8 %copy-start.2 = (f32[128]{0:T(128)S(1)}, f32[128]{0:T(128)}, u32[]{:S(2)}) copy-start(f32[128]{0:T(128)} %param.22) | copy-start | bytes 1540
  0.1 41.8 %copy-start = (f32[1,4096]{1,0:T(1,128)S(1)}, f32[1,4096]{1,0:T(1,128)}, u32[]{:S(2)}) copy-start(f32[1,4096]{1,0:T(1,128)} %param.21) | copy-start | bytes 49156
  0.1 15.8 %copy-start.15 = (s32[2,2,2048]{2,1,0:T(2,128)S(1)}, s32[2,2,2048]{2,1,0:T(2,128)}, u32[]{:S(2)}) copy-start(s32[2,2,2048]{2,1,0:T(2,128)} %param.25) | copy-start | bytes 98308
  0.2 15.8 %copy-start.14 = (f32[2,2048]{1,0:T(2,128)S(1)}, f32[2,2048]{1,0:T(2,128)}, u32[]{:S(2)}) copy-start(f32[2,2048]{1,0:T(2,128)} %param.24) | copy-start | bytes 49156
  5.9 19.2 %all-to-all-start = ((f32[16,64,128]{2,1,0:T(8,128)}), f32[16,64,128]{2,1,0:T(8,128)S(1)}, u32[]{:S(2)}, u32[]{:S(2)}) async-start(f32[16,64,128]{2,1,0:T(8,128)} %forward.1), calls=%async_computation | async-start | bytes 1048576 | tf_op jit(solution)/shard_map/all_to_all | solution.py:435
  16.0 7.5 %collective-permute-start = (f32[4,16,128]{2,1,0:T(8,128)S(1)}, f32[4,16,128]{2,1,0:T(8,128)S(1)}, u32[]{:S(2)}, u32[]{:S(2)}) collective-permute-start(f32[4,16,128]{2,1,0:T(8,128)S(1)} %bitcast.16), channel_id=1, source_target_pairs={{0,0},{1,1},{2,2},{3,3},{4,4},{5,5},{6,6},{7,7},{9,8},{8,9},{11,10... | collective-permute-start | bytes 98312 | tf_op jit(solution)/shard_map/ppermute | solution.py:452
  23.5 1.2 %collective-permute-start.1 = (f32[4,16,128]{2,1,0:T(8,128)S(1)}, f32[4,16,128]{2,1,0:T(8,128)S(1)}, u32[]{:S(2)}, u32[]{:S(2)}) collective-permute-start(f32[4,16,128]{2,1,0:T(8,128)S(1)} %collective-permute-done.own), channel_id=1, source_target_pairs={{0,8},{8,0},{16,24},{24,16},{32,40},{40,32},{48,56},{56,48},{64,72... | collective-permute-start | bytes 98312 | tf_op jit(solution)/shard_map/ppermute | solution.py:453

commit v5 on v4

--- a/solution.py
+++ b/solution.py
@@ -234,7 +234,7 @@
             out[1, at + w] = jnp.sin(src[planes + w])
 
 
-def middle_kernel(place, x, ready, tw_cos, tw_sin, fwd_hi, fwd_lo, bwd_hi, bwd_lo, out, br, bi, qr, qi):
+def middle_kernel(place, place_b, x, ready, tw_cos, tw_sin, fwd_hi, fwd_lo, bwd_hi, bwd_lo, out, br, bi, qr, qi):
     outer = x.shape[0]
     rows = x.shape[1] // 2
     groups = rows // 8
@@ -264,7 +264,7 @@
         for a in range(outer):
             c, s = ready[0, w, a : a + 1, :], ready[1, w, a : a + 1, :]
             hr, hi = re[a] * c + im[a] * s, im[a] * c - re[a] * s
-            to = place[a]
+            to = place_b[a]
             if w == 0:
                 out[to, top, :] = hr
                 out[to, bot, :] = hi
@@ -412,8 +412,10 @@
     return pl.CostEstimate(flops=flops, bytes_accessed=nbytes, transcendentals=0)
 
 
-def exchange_order(count):
-    return list(range(count - 1, -1, -1))
+def exchange_orders():
+    first = [4 * x + 2 * z + c for x in (3, 2, 0, 1) for z in (1, 0) for c in (1, 0)]
+    second = [4 * x + 2 * z + c for z in (1, 0) for x in (2, 3, 1, 0) for c in (1, 0)]
+    return first, second
 
 
 def on_device(facets, correction, window, offsets, phases, coverage):
@@ -428,10 +430,11 @@
     per_owner = coverage.shape[0]
     width = facet_count * LANES
 
-    members = exchange_order(facet_count)
+    members, members_b = exchange_orders()
     place = [members.index(f) for f in range(facet_count)]
-
-    def exchange(blocks):
+    place_b = [members_b.index(f) for f in range(facet_count)]
+
+    def exchange(blocks, members):
         return lax.all_to_all(blocks, "facet", split_axis=0, concat_axis=0, tiled=True, axis_index_groups=[members])
 
 
@@ -498,14 +501,14 @@
         cost_estimate=cost(10**9, 10**7),
         name="forward",
     )(offsets, facets.reshape(facets.shape[1:]), corr, tw_both, line, block, window)
-    got = exchange(sent)
+    got = exchange(sent, members)
 
     tw2 = trig(facet_count, LANES, width)
     fwd_hi, fwd_lo = halves(np.block([[c128, -s128], [s128, c128]]))
     inverse = np.block([[c128, s128], [-s128, c128]])
     bwd_hi, bwd_lo = halves(inverse * (1.0 / (width * WPLANES)))
     adjoint = pl.pallas_call(
-        lambda *refs: middle_kernel(place, *refs),
+        lambda *refs: middle_kernel(place, place_b, *refs),
         in_specs=[vmem()] * 8,
         out_specs=vmem(),
         scratch_shapes=[pltpu.VMEM((2, facet_count, half, LANES), F32)] * 4,
@@ -514,11 +517,11 @@
         cost_estimate=cost(10**9, 10**7),
         name="middle",
     )(got, ready, jnp.asarray(tw2[0], F32), jnp.asarray(tw2[1], F32), fwd_hi, fwd_lo, bwd_hi, bwd_lo)
-    back = exchange(adjoint)
+    back = exchange(adjoint, members_b)
 
     line_hi, line_lo = halves(inverse * length**-0.5)
     result = pl.pallas_call(
-        lambda *refs: backward_kernel(sub_count, per_owner, place, *refs),
+        lambda *refs: backward_kernel(sub_count, per_owner, place_b, *refs),
         in_specs=[smem()] + [vmem()] * 8,
         out_specs=hbm(),
         scratch_shapes=[

time: 46.8 us -> 46.1 us (0.985)
  no operation moved by 1% of the time
where the time goes in v5:
time: 46.1 us; the launch traced here: 45.8 us
  Pallas kernels  13.8 us (30%)
  blocking collectives  13.3 us (29%)
  starting transfers between devices  12.7 us (28%)
  waiting for transfers between devices  5.58 us (12%)
    all_to_all x1, blocking collectives, exchange(): lax.all_to_all(blocks, 'facet', split_axis=0, concat_axis=0, tiled=True,...  13.3 us
    all_to_all x1, starting transfers between devices, exchange(): lax.all_to_all(blocks, 'facet', split_axis=0, concat_axis=0, tiled=True,...  10 us
    pallas_call x1, Pallas kernels, on_device(): pl.pallas_call(lambda *refs: forward_kernel(sub_count, pair_count, per_ow...  5.73 us
    pallas_call x1, Pallas kernels, on_device(): pl.pallas_call(lambda *refs: backward_kernel(sub_count, per_owner, place_...  4.52 us
    ppermute x1, waiting for transfers between devices, on_device(): fetched = lax.ppermute(payload, names, route)  4.38 us
    pallas_call x1, Pallas kernels, on_device(): pl.pallas_call(lambda *refs: middle_kernel(place, place_b, *refs), in_spe...  3.19 us
    ppermute x1, starting transfers between devices, on_device(): fetched = lax.ppermute(payload, names, route)  2.65 us
    ppermute x1, waiting for transfers between devices, on_device(): lax.ppermute(fetched, 'facet', [(f, f ^ 1) for f in range(facet_count)])  1.2 us
  transfers between devices with their start and end apart: 3, of which 2 were waited for; matrix products, arithmetic and copies ran while one was open for 0% of the time, Pallas kernels for 1%

profile of v5, /device:TPU:1, one launch (start us, length us, event | category | flops | bytes accessed | tf_op | source)
XLA Modules:
  0.0 45.8 jit_solution(9072814961240030429)
XLA Ops:
  0.0 0.0 copy-start.12
  0.0 0.0 copy-start.13
  0.0 0.0 copy-start.6
  0.0 0.0 copy-start.7
  0.0 0.0 copy-start.8
  0.0 0.0 copy-start.9
  0.0 0.0 copy-start.3
  0.1 0.0 copy-start.4
  0.1 0.0 copy-start.5
  0.1 0.0 copy-start.10
  0.1 0.0 copy-start.11
  0.1 0.0 copy-start.1
  0.1 0.0 copy-start.2
  0.1 0.0 copy-start
  0.1 0.0 copy-start.15
  0.2 0.0 copy-start.14
  0.2 5.7 %forward.1 = f32[16,64,128]{2,1,0:T(8,128)} custom-call(s32[8]{0:T(128)} %refs_0_.3, f32[512,2,4096]{2,1,0:T(2,128)} %bitcast.15, f32[32,128]{1,0:T(8,128)} %bitcast.11, f32[64,128]{1,0:T(8,128)} %constant.64.clone.refs_3_, bf16[2,256,256]{2,1,0:T(8,128)(2,1)} %constant.65.clone.refs_4_, f32[128,256]{1,0:T(8,128)} %constant.66.clone.refs_5_, f32[1,128]{1,0:T(1,128)} %bitcast.13), custom_call_target="tpu_custom_call" | custom-call | flops 1000000000 | bytes 10000000 | tf_op jit(solution)/shard_map/forward/pallas_call | solution.py:479
  5.9 10.0 %all-to-all-start = ((f32[16,64,128]{2,1,0:T(8,128)}), f32[16,64,128]{2,1,0:T(8,128)S(1)}, u32[]{:S(2)}, u32[]{:S(2)}) async-start(f32[16,64,128]{2,1,0:T(8,128)} %forward.1), calls=%async_computation | async-start | bytes 1048576 | tf_op jit(solution)/shard_map/all_to_all | solution.py:438
  15.9 0.0 copy-done.15
  16.0 0.0 copy-done.14
  16.0 2.7 %collective-permute-start = (f32[4,16,128]{2,1,0:T(8,128)S(1)}, f32[4,16,128]{2,1,0:T(8,128)S(1)}, u32[]{:S(2)}, u32[]{:S(2)}) collective-permute-start(f32[4,16,128]{2,1,0:T(8,128)S(1)} %bitcast.16), channel_id=1, source_target_pairs={{0,0},{1,1},{2,2},{3,3},{4,4},{5,5},{6,6},{7,7},{9,8},{8,9},{11,10... | collective-permute-start | bytes 98312 | tf_op jit(solution)/shard_map/ppermute | solution.py:455
  18.7 4.4 %collective-permute-done.own = f32[4,16,128]{2,1,0:T(8,128)S(1)} collective-permute-done((f32[4,16,128]{2,1,0:T(8,128)S(1)}, f32[4,16,128]{2,1,0:T(8,128)S(1)}, u32[]{:S(2)}, u32[]{:S(2)}) %collective-permute-start) | collective-permute-done | bytes 32800 | tf_op jit(solution)/shard_map/ppermute | solution.py:455
  23.0 0.0 collective-permute-start.1
  23.1 1.2 %collective-permute-done.1.other = f32[4,16,128]{2,1,0:T(8,128)S(1)} collective-permute-done((f32[4,16,128]{2,1,0:T(8,128)S(1)}, f32[4,16,128]{2,1,0:T(8,128)S(1)}, u32[]{:S(2)}, u32[]{:S(2)}) %collective-permute-start.1) | collective-permute-done | bytes 32800 | tf_op jit(solution)/shard_map/ppermute | solution.py:456
  24.3 0.4 ready.1.refs_1_
  24.7 0.0 all-to-all-done.refs_0_
  24.7 0.0 copy-done.12
  24.7 0.0 copy-done.13
  24.7 0.0 copy-done.6
  24.7 0.0 copy-done.7
  24.7 0.0 copy-done.8
  24.7 0.0 copy-done.9
  24.7 3.2 %middle.1 = f32[16,64,128]{2,1,0:T(8,128)S(1)} custom-call(f32[16,64,128]{2,1,0:T(8,128)S(1)} %all-to-all-done.refs_0_, f32[3,4,16,128]{3,2,1,0:T(8,128)S(1)} %ready.1.refs_1_, f32[16,128]{1,0:T(8,128)S(1)} %copy-done.13, f32[16,128]{1,0:T(8,128)S(1)} %copy-done.12, bf16[256,256]{1,0:T(8,128)(2,1)S(1)} %copy-done.9, bf16[256,256]{1,0:T(8,128)(2,1)S(1)} %copy-done.8, ...), custom_call_target="tpu_custom_call" | custom-call | flops 1000000000 | bytes 10000000 | tf_op jit(solution)/shard_map/middle/pallas_call | solution.py:510
  27.9 13.3 %all_to_all.10.refs_1_ = f32[16,64,128]{2,1,0:T(8,128)S(1)} all-to-all(f32[16,64,128]{2,1,0:T(8,128)S(1)} %middle.1), channel_id=1, replica_groups={{88,80,120,112,56,48,24,16,72,64,104,96,40,32,8,0},{89,81,121,113,57,49..., dimensions={0} | all-to-all | bytes 1048576 | tf_op jit(solution)/shard_map/all_to_all | solution.py:438
  41.2 0.0 copy-done.3
  41.2 0.0 copy-done.4
  41.2 0.0 copy-done.5
  41.2 0.0 copy-done.10
  41.3 0.0 copy-done.11
  41.3 0.0 copy-done.1
  41.3 0.0 copy-done.2
  41.3 0.0 copy-done
  41.3 4.5 %backward.1 = f32[64,2,4096]{2,1,0:T(2,128)} custom-call(s32[8]{0:T(128)S(1)} %copy-done.1, f32[16,64,128]{2,1,0:T(8,128)S(1)} %all_to_all.10.refs_1_, f32[32,128]{1,0:T(8,128)S(1)} %bitcast.12, f32[32,128]{1,0:T(8,128)S(1)} %copy-done.11, f32[32,128]{1,0:T(8,128)S(1)} %copy-done.10, f32[128,256]{1,0:T(8,128)S(1)} %copy-done.5, f32[1,128]{1,0:T(1,128)S(1)} %bitcast.14, ...), custom_call_target="tpu_custom_call" | custom-call | flops 1000000000 | bytes 10000000 | tf_op jit(solution)/shard_map/backward/pallas_call | solution.py:523
  (3 shorter events, 0.0 us)
Async XLA Ops:
  0.0 24.7 %copy-start.12 = (f32[16,128]{1,0:T(8,128)S(1)}, f32[16,128]{1,0:T(8,128)}, u32[]{:S(2)}) copy-start(f32[16,128]{1,0:T(8,128)} %constant.73.clone.refs_3_) | copy-start | bytes 24580
  0.0 24.7 %copy-start.13 = (f32[16,128]{1,0:T(8,128)S(1)}, f32[16,128]{1,0:T(8,128)}, u32[]{:S(2)}) copy-start(f32[16,128]{1,0:T(8,128)} %constant.72.clone.refs_2_) | copy-start | bytes 24580
  0.0 24.7 %copy-start.6 = (bf16[256,256]{1,0:T(8,128)(2,1)S(1)}, bf16[256,256]{1,0:T(8,128)(2,1)}, u32[]{:S(2)}) copy-start(bf16[256,256]{1,0:T(8,128)(2,1)} %constant.71.clone.refs_7_) | copy-start | bytes 393220
  0.0 24.7 %copy-start.7 = (bf16[256,256]{1,0:T(8,128)(2,1)S(1)}, bf16[256,256]{1,0:T(8,128)(2,1)}, u32[]{:S(2)}) copy-start(bf16[256,256]{1,0:T(8,128)(2,1)} %constant.70.clone.refs_6_) | copy-start | bytes 393220
  0.0 24.7 %copy-start.8 = (bf16[256,256]{1,0:T(8,128)(2,1)S(1)}, bf16[256,256]{1,0:T(8,128)(2,1)}, u32[]{:S(2)}) copy-start(bf16[256,256]{1,0:T(8,128)(2,1)} %constant.69.clone.refs_5_) | copy-start | bytes 393220
  0.0 24.7 %copy-start.9 = (bf16[256,256]{1,0:T(8,128)(2,1)S(1)}, bf16[256,256]{1,0:T(8,128)(2,1)}, u32[]{:S(2)}) copy-start(bf16[256,256]{1,0:T(8,128)(2,1)} %constant.68.clone.refs_4_) | copy-start | bytes 393220
  0.0 41.2 %copy-start.3 = (bf16[256,256]{1,0:T(8,128)(2,1)S(1)}, bf16[256,256]{1,0:T(8,128)(2,1)}, u32[]{:S(2)}) copy-start(bf16[256,256]{1,0:T(8,128)(2,1)} %constant.75.clone.refs_8_) | copy-start | bytes 393220
  0.1 41.2 %copy-start.4 = (bf16[256,256]{1,0:T(8,128)(2,1)S(1)}, bf16[256,256]{1,0:T(8,128)(2,1)}, u32[]{:S(2)}) copy-start(bf16[256,256]{1,0:T(8,128)(2,1)} %constant.74.clone.refs_7_) | copy-start | bytes 393220
  0.1 41.2 %copy-start.5 = (f32[128,256]{1,0:T(8,128)S(1)}, f32[128,256]{1,0:T(8,128)}, u32[]{:S(2)}) copy-start(f32[128,256]{1,0:T(8,128)} %constant.67.clone.refs_5_) | copy-start | bytes 393220
  0.1 41.2 %copy-start.10 = (f32[32,128]{1,0:T(8,128)S(1)}, f32[32,128]{1,0:T(8,128)}, u32[]{:S(2)}) copy-start(f32[32,128]{1,0:T(8,128)} %constant.63.clone.refs_4_) | copy-start | bytes 49156
  0.1 41.2 %copy-start.11 = (f32[32,128]{1,0:T(8,128)S(1)}, f32[32,128]{1,0:T(8,128)}, u32[]{:S(2)}) copy-start(f32[32,128]{1,0:T(8,128)} %constant.62.clone.refs_3_) | copy-start | bytes 49156
  0.1 41.2 %copy-start.1 = (s32[8]{0:T(128)S(1)}, s32[8]{0:T(128)}, u32[]{:S(2)}) copy-start(s32[8]{0:T(128)} %refs_0_.3) | copy-start | bytes 100
  0.1 41.2 %copy-start.2 = (f32[128]{0:T(128)S(1)}, f32[128]{0:T(128)}, u32[]{:S(2)}) copy-start(f32[128]{0:T(128)} %param.22) | copy-start | bytes 1540
  0.1 41.2 %copy-start = (f32[1,4096]{1,0:T(1,128)S(1)}, f32[1,4096]{1,0:T(1,128)}, u32[]{:S(2)}) copy-start(f32[1,4096]{1,0:T(1,128)} %param.21) | copy-start | bytes 49156
  0.1 15.8 %copy-start.15 = (s32[2,2,2048]{2,1,0:T(2,128)S(1)}, s32[2,2,2048]{2,1,0:T(2,128)}, u32[]{:S(2)}) copy-start(s32[2,2,2048]{2,1,0:T(2,128)} %param.25) | copy-start | bytes 98308
  0.2 15.8 %copy-start.14 = (f32[2,2048]{1,0:T(2,128)S(1)}, f32[2,2048]{1,0:T(2,128)}, u32[]{:S(2)}) copy-start(f32[2,2048]{1,0:T(2,128)} %param.24) | copy-start | bytes 49156
  5.9 18.8 %all-to-all-start = ((f32[16,64,128]{2,1,0:T(8,128)}), f32[16,64,128]{2,1,0:T(8,128)S(1)}, u32[]{:S(2)}, u32[]{:S(2)}) async-start(f32[16,64,128]{2,1,0:T(8,128)} %forward.1), calls=%async_computation | async-start | bytes 1048576 | tf_op jit(solution)/shard_map/all_to_all | solution.py:438
  16.0 7.0 %collective-permute-start = (f32[4,16,128]{2,1,0:T(8,128)S(1)}, f32[4,16,128]{2,1,0:T(8,128)S(1)}, u32[]{:S(2)}, u32[]{:S(2)}) collective-permute-start(f32[4,16,128]{2,1,0:T(8,128)S(1)} %bitcast.16), channel_id=1, source_target_pairs={{0,0},{1,1},{2,2},{3,3},{4,4},{5,5},{6,6},{7,7},{9,8},{8,9},{11,10... | collective-permute-start | bytes 98312 | tf_op jit(solution)/shard_map/ppermute | solution.py:455
  23.0 1.2 %collective-permute-start.1 = (f32[4,16,128]{2,1,0:T(8,128)S(1)}, f32[4,16,128]{2,1,0:T(8,128)S(1)}, u32[]{:S(2)}, u32[]{:S(2)}) collective-permute-start(f32[4,16,128]{2,1,0:T(8,128)S(1)} %collective-permute-done.own), channel_id=1, source_target_pairs={{0,8},{8,0},{16,24},{24,16},{32,40},{40,32},{48,56},{56,48},{64,72... | collective-permute-start | bytes 98312 | tf_op jit(solution)/shard_map/ppermute | solution.py:456

commit v6 on v5

--- a/solution.py
+++ b/solution.py
@@ -176,7 +176,7 @@
     for c in tables[2:]:
         c.wait()
 
-    per_step = 8
+    per_step = 4
     for j in range(outer // per_step):
         ks = range(j * per_step, (j + 1) * per_step)
         left = jnp.concatenate([yr[k] for k in ks], 0)
@@ -216,8 +216,8 @@
         c.wait()
 
 
-def ready_kernel(own, other, out):
-    planes, outer = own.shape[0] // 2, own.shape[1]
+def ready_kernel(src, out):
+    planes, outer = src.shape[0] // 2, src.shape[1]
     per = LANES // outer
     row = lax.broadcasted_iota(jnp.int32, (LANES, LANES), 0)
     lane = lax.broadcasted_iota(jnp.int32, (LANES, LANES), 1)
@@ -226,19 +226,20 @@
     short_lane = lax.broadcasted_iota(jnp.int32, (outer, LANES), 1)
     spread = (short_lane // per == short_row).astype(F32).astype(BF16)
     fold = (short_lane % outer == short_row).astype(F32).astype(BF16)
-    for src, at in ((own, 0), (other, planes)):
-        for w in range(planes):
-            wide = dot_nn(src[w].T.astype(BF16), spread)
-            out[2, at + w] = dot_nn(fold, jnp.where(mask, wide, 0.0).astype(BF16))
-            out[0, at + w] = jnp.cos(src[planes + w])
-            out[1, at + w] = jnp.sin(src[planes + w])
-
-
-def middle_kernel(place, place_b, x, ready, tw_cos, tw_sin, fwd_hi, fwd_lo, bwd_hi, bwd_lo, out, br, bi, qr, qi):
+    for w in range(planes):
+        wide = dot_nn(src[w].T.astype(BF16), spread)
+        out[2, w] = dot_nn(fold, jnp.where(mask, wide, 0.0).astype(BF16))
+        out[0, w] = jnp.cos(src[planes + w])
+        out[1, w] = jnp.sin(src[planes + w])
+
+
+def middle_kernel(place, place_b, x, ready_a, ready_b, tw_cos, tw_sin, fwd_hi, fwd_lo, bwd_hi, bwd_lo, out, br, bi, qr, qi):
     outer = x.shape[0]
     rows = x.shape[1] // 2
     groups = rows // 8
-    planes = ready.shape[1]
+    planes = 2 * ready_a.shape[1]
+    ready = (ready_a, ready_b)
+    each = ready_a.shape[1]
     parts = 2
     step = outer // parts
 
@@ -246,7 +247,7 @@
         top, bot = slice(g * 8, g * 8 + 8), slice(rows + g * 8, rows + g * 8 + 8)
         re, im = [], []
         for a in range(outer):
-            c, s = ready[0, w, a : a + 1, :], ready[1, w, a : a + 1, :]
+            c, s = ready[w // each][0, w % each, a : a + 1, :], ready[w // each][1, w % each, a : a + 1, :]
             p, q = x[place[a], top, :], x[place[a], bot, :]
             re.append(p * c - q * s)
             im.append(p * s + q * c)
@@ -262,7 +263,7 @@
         im = [qi[w % 2, k, top, :] for k in range(outer)]
         re, im = small_fft(re, im, 1.0)
         for a in range(outer):
-            c, s = ready[0, w, a : a + 1, :], ready[1, w, a : a + 1, :]
+            c, s = ready[w // each][0, w % each, a : a + 1, :], ready[w // each][1, w % each, a : a + 1, :]
             hr, hi = re[a] * c + im[a] * s, im[a] * c - re[a] * s
             to = place_b[a]
             if w == 0:
@@ -281,7 +282,7 @@
     def from_grid(w, part, g):
         scaled = []
         for e in range(step):
-            row = ready[2, w, part * step + e : part * step + e + 1, :]
+            row = ready[w // each][2, w % each, part * step + e : part * step + e + 1, :]
             piece = g[e * rows : (e + 1) * rows]
             scaled.append(jnp.concatenate([piece[:, :LANES] * row, piece[:, LANES:] * row], 1))
         q = product(jnp.concatenate(scaled, 0), bwd_hi[...], bwd_lo[...])
@@ -454,15 +455,16 @@
                 route.append((number(*source), number(f, y, w)))
     fetched = lax.ppermute(payload, names, route)
     swapped = lax.ppermute(fetched, "facet", [(f, f ^ 1) for f in range(facet_count)])
-    ready = pl.pallas_call(
+    make_ready = pl.pallas_call(
         ready_kernel,
-        in_specs=[vmem()] * 2,
+        in_specs=[vmem()],
         out_specs=vmem(),
-        out_shape=jax.ShapeDtypeStruct((3, WPLANES, facet_count, LANES), F32),
+        out_shape=jax.ShapeDtypeStruct((3, WPLANES // pair_count, facet_count, LANES), F32),
         compiler_params=params(4),
         cost_estimate=cost(10**7, 10**6),
         name="ready",
-    )(fetched, swapped)
+    )
+    ready = make_ready(fetched), make_ready(swapped)
 
     tw = trig(outer, LANES, length)
     tw_cos, tw_sin = jnp.asarray(tw[0], F32), jnp.asarray(tw[1], F32)
@@ -509,14 +511,14 @@
     bwd_hi, bwd_lo = halves(inverse * (1.0 / (width * WPLANES)))
     adjoint = pl.pallas_call(
         lambda *refs: middle_kernel(place, place_b, *refs),
-        in_specs=[vmem()] * 8,
+        in_specs=[vmem()] * 9,
         out_specs=vmem(),
         scratch_shapes=[pltpu.VMEM((2, facet_count, half, LANES), F32)] * 4,
         out_shape=jax.ShapeDtypeStruct((facet_count, rows, LANES), F32),
         compiler_params=params(12),
         cost_estimate=cost(10**9, 10**7),
         name="middle",
-    )(got, ready, jnp.asarray(tw2[0], F32), jnp.asarray(tw2[1], F32), fwd_hi, fwd_lo, bwd_hi, bwd_lo)
+    )(got, *ready, jnp.asarray(tw2[0], F32), jnp.asarray(tw2[1], F32), fwd_hi, fwd_lo, bwd_hi, bwd_lo)
     back = exchange(adjoint, members_b)
 
     line_hi, line_lo = halves(inverse * length**-0.5)

time: 46.1 us -> 46 us (level)
  transfers between devices with their start and end apart: 3 -> 3, of which waited for: 2 -> 2; matrix products, arithmetic and copies ran while one was open for 0% -> 0% of each run, Pallas kernels for 1% -> 2%
where the time goes in v6:
time: 46 us; the launch traced here: 45.7 us
  Pallas kernels  14 us (30%)
  blocking collectives  13.3 us (29%)
  starting transfers between devices  12.7 us (28%)
  waiting for transfers between devices  5.24 us (11%)
    all_to_all x1, blocking collectives, exchange(): lax.all_to_all(blocks, 'facet', split_axis=0, concat_axis=0, tiled=True,...  13.3 us
    all_to_all x1, starting transfers between devices, exchange(): lax.all_to_all(blocks, 'facet', split_axis=0, concat_axis=0, tiled=True,...  10 us
    pallas_call x1, Pallas kernels, on_device(): pl.pallas_call(lambda *refs: forward_kernel(sub_count, pair_count, per_ow...  5.66 us
    pallas_call x1, Pallas kernels, on_device(): pl.pallas_call(lambda *refs: backward_kernel(sub_count, per_owner, place_...  4.52 us
    ppermute x1, waiting for transfers between devices, on_device(): fetched = lax.ppermute(payload, names, route)  4.38 us
    pallas_call x1, Pallas kernels, on_device(): pl.pallas_call(lambda *refs: middle_kernel(place, place_b, *refs), in_spe...  3.18 us
    ppermute x1, starting transfers between devices, on_device(): fetched = lax.ppermute(payload, names, route)  2.65 us
  transfers between devices with their start and end apart: 3, of which 2 were waited for; matrix products, arithmetic and copies ran while one was open for 0% of the time, Pallas kernels for 2%

profile of v6, /device:TPU:1, one launch (start us, length us, event | category | flops | bytes accessed | tf_op | source)
XLA Modules:
  0.0 45.7 jit_solution(10066225202259674501)
XLA Ops:
  0.0 0.0 copy-start.12
  0.0 0.0 copy-start.13
  0.0 0.0 copy-start.6
  0.0 0.0 copy-start.7
  0.0 0.0 copy-start.8
  0.0 0.0 copy-start.9
  0.0 0.0 copy-start.3
  0.1 0.0 copy-start.4
  0.1 0.0 copy-start.5
  0.1 0.0 copy-start.10
  0.1 0.0 copy-start.11
  0.1 0.0 copy-start.1
  0.1 0.0 copy-start.2
  0.1 0.0 copy-start
  0.1 0.0 copy-start.15
  0.2 0.0 copy-start.14
  0.2 5.7 %forward.1 = f32[16,64,128]{2,1,0:T(8,128)} custom-call(s32[8]{0:T(128)} %refs_0_.3, f32[512,2,4096]{2,1,0:T(2,128)} %bitcast.15, f32[32,128]{1,0:T(8,128)} %bitcast.11, f32[64,128]{1,0:T(8,128)} %constant.64.clone.refs_3_, bf16[2,256,256]{2,1,0:T(8,128)(2,1)} %constant.65.clone.refs_4_, f32[128,256]{1,0:T(8,128)} %constant.66.clone.refs_5_, f32[1,128]{1,0:T(1,128)} %bitcast.13), custom_call_target="tpu_custom_call" | custom-call | flops 1000000000 | bytes 10000000 | tf_op jit(solution)/shard_map/forward/pallas_call | solution.py:481
  5.8 10.0 %all-to-all-start = ((f32[16,64,128]{2,1,0:T(8,128)}), f32[16,64,128]{2,1,0:T(8,128)S(1)}, u32[]{:S(2)}, u32[]{:S(2)}) async-start(f32[16,64,128]{2,1,0:T(8,128)} %forward.1), calls=%async_computation | async-start | bytes 1048576 | tf_op jit(solution)/shard_map/all_to_all | solution.py:439
  15.9 0.0 copy-done.15
  15.9 0.0 copy-done.14
  16.0 2.6 %collective-permute-start = (f32[4,16,128]{2,1,0:T(8,128)S(1)}, f32[4,16,128]{2,1,0:T(8,128)S(1)}, u32[]{:S(2)}, u32[]{:S(2)}) collective-permute-start(f32[4,16,128]{2,1,0:T(8,128)S(1)} %bitcast.16), channel_id=1, source_target_pairs={{0,0},{1,1},{2,2},{3,3},{4,4},{5,5},{6,6},{7,7},{9,8},{8,9},{11,10... | collective-permute-start | bytes 98312 | tf_op jit(solution)/shard_map/ppermute | solution.py:456
  18.6 4.4 %collective-permute-done.src = f32[4,16,128]{2,1,0:T(8,128)S(1)} collective-permute-done((f32[4,16,128]{2,1,0:T(8,128)S(1)}, f32[4,16,128]{2,1,0:T(8,128)S(1)}, u32[]{:S(2)}, u32[]{:S(2)}) %collective-permute-start) | collective-permute-done | bytes 32800 | tf_op jit(solution)/shard_map/ppermute | solution.py:456
  23.0 0.0 collective-permute-start.1
  23.0 0.3 ready.2.refs_1_
  23.3 0.9 %collective-permute-done.1.src = f32[4,16,128]{2,1,0:T(8,128)S(1)} collective-permute-done((f32[4,16,128]{2,1,0:T(8,128)S(1)}, f32[4,16,128]{2,1,0:T(8,128)S(1)}, u32[]{:S(2)}, u32[]{:S(2)}) %collective-permute-start.1) | collective-permute-done | bytes 32800 | tf_op jit(solution)/shard_map/ppermute | solution.py:457
  24.2 0.3 ready.3.refs_2_
  24.5 0.0 all-to-all-done.refs_0_
  24.5 0.0 copy-done.12
  24.5 0.0 copy-done.13
  24.6 0.0 copy-done.6
  24.6 0.0 copy-done.7
  24.6 0.0 copy-done.8
  24.6 0.0 copy-done.9
  24.6 3.2 %middle.1 = f32[16,64,128]{2,1,0:T(8,128)S(1)} custom-call(f32[16,64,128]{2,1,0:T(8,128)S(1)} %all-to-all-done.refs_0_, f32[3,2,16,128]{3,2,1,0:T(8,128)S(1)} %ready.2.refs_1_, f32[3,2,16,128]{3,2,1,0:T(8,128)S(1)} %ready.3.refs_2_, f32[16,128]{1,0:T(8,128)S(1)} %copy-done.13, f32[16,128]{1,0:T(8,128)S(1)} %copy-done.12, bf16[256,256]{1,0:T(8,128)(2,1)S(1)} %copy-done.9, ...), custom_call_target="tpu_custom_call" | custom-call | flops 1000000000 | bytes 10000000 | tf_op jit(solution)/shard_map/middle/pallas_call | solution.py:512
  27.8 13.3 %all_to_all.10.refs_1_ = f32[16,64,128]{2,1,0:T(8,128)S(1)} all-to-all(f32[16,64,128]{2,1,0:T(8,128)S(1)} %middle.1), channel_id=1, replica_groups={{88,80,120,112,56,48,24,16,72,64,104,96,40,32,8,0},{89,81,121,113,57,49..., dimensions={0} | all-to-all | bytes 1048576 | tf_op jit(solution)/shard_map/all_to_all | solution.py:439
  41.1 0.0 copy-done.3
  41.1 0.0 copy-done.4
  41.1 0.0 copy-done.5
  41.1 0.0 copy-done.10
  41.1 0.0 copy-done.11
  41.1 0.0 copy-done.1
  41.1 0.0 copy-done.2
  41.2 0.0 copy-done
  41.2 4.5 %backward.1 = f32[64,2,4096]{2,1,0:T(2,128)} custom-call(s32[8]{0:T(128)S(1)} %copy-done.1, f32[16,64,128]{2,1,0:T(8,128)S(1)} %all_to_all.10.refs_1_, f32[32,128]{1,0:T(8,128)S(1)} %bitcast.12, f32[32,128]{1,0:T(8,128)S(1)} %copy-done.11, f32[32,128]{1,0:T(8,128)S(1)} %copy-done.10, f32[128,256]{1,0:T(8,128)S(1)} %copy-done.5, f32[1,128]{1,0:T(1,128)S(1)} %bitcast.14, ...), custom_call_target="tpu_custom_call" | custom-call | flops 1000000000 | bytes 10000000 | tf_op jit(solution)/shard_map/backward/pallas_call | solution.py:525
  (3 shorter events, 0.0 us)
Async XLA Ops:
  0.0 24.5 %copy-start.12 = (f32[16,128]{1,0:T(8,128)S(1)}, f32[16,128]{1,0:T(8,128)}, u32[]{:S(2)}) copy-start(f32[16,128]{1,0:T(8,128)} %constant.73.clone.refs_4_) | copy-start | bytes 24580
  0.0 24.5 %copy-start.13 = (f32[16,128]{1,0:T(8,128)S(1)}, f32[16,128]{1,0:T(8,128)}, u32[]{:S(2)}) copy-start(f32[16,128]{1,0:T(8,128)} %constant.72.clone.refs_3_) | copy-start | bytes 24580
  0.0 24.6 %copy-start.6 = (bf16[256,256]{1,0:T(8,128)(2,1)S(1)}, bf16[256,256]{1,0:T(8,128)(2,1)}, u32[]{:S(2)}) copy-start(bf16[256,256]{1,0:T(8,128)(2,1)} %constant.71.clone.refs_8_) | copy-start | bytes 393220
  0.0 24.6 %copy-start.7 = (bf16[256,256]{1,0:T(8,128)(2,1)S(1)}, bf16[256,256]{1,0:T(8,128)(2,1)}, u32[]{:S(2)}) copy-start(bf16[256,256]{1,0:T(8,128)(2,1)} %constant.70.clone.refs_7_) | copy-start | bytes 393220
  0.0 24.6 %copy-start.8 = (bf16[256,256]{1,0:T(8,128)(2,1)S(1)}, bf16[256,256]{1,0:T(8,128)(2,1)}, u32[]{:S(2)}) copy-start(bf16[256,256]{1,0:T(8,128)(2,1)} %constant.69.clone.refs_6_) | copy-start | bytes 393220
  0.0 24.6 %copy-start.9 = (bf16[256,256]{1,0:T(8,128)(2,1)S(1)}, bf16[256,256]{1,0:T(8,128)(2,1)}, u32[]{:S(2)}) copy-start(bf16[256,256]{1,0:T(8,128)(2,1)} %constant.68.clone.refs_5_) | copy-start | bytes 393220
  0.0 41.1 %copy-start.3 = (bf16[256,256]{1,0:T(8,128)(2,1)S(1)}, bf16[256,256]{1,0:T(8,128)(2,1)}, u32[]{:S(2)}) copy-start(bf16[256,256]{1,0:T(8,128)(2,1)} %constant.75.clone.refs_8_) | copy-start | bytes 393220
  0.1 41.0 %copy-start.4 = (bf16[256,256]{1,0:T(8,128)(2,1)S(1)}, bf16[256,256]{1,0:T(8,128)(2,1)}, u32[]{:S(2)}) copy-start(bf16[256,256]{1,0:T(8,128)(2,1)} %constant.74.clone.refs_7_) | copy-start | bytes 393220
  0.1 41.0 %copy-start.5 = (f32[128,256]{1,0:T(8,128)S(1)}, f32[128,256]{1,0:T(8,128)}, u32[]{:S(2)}) copy-start(f32[128,256]{1,0:T(8,128)} %constant.67.clone.refs_5_) | copy-start | bytes 393220
  0.1 41.0 %copy-start.10 = (f32[32,128]{1,0:T(8,128)S(1)}, f32[32,128]{1,0:T(8,128)}, u32[]{:S(2)}) copy-start(f32[32,128]{1,0:T(8,128)} %constant.63.clone.refs_4_) | copy-start | bytes 49156
  0.1 41.0 %copy-start.11 = (f32[32,128]{1,0:T(8,128)S(1)}, f32[32,128]{1,0:T(8,128)}, u32[]{:S(2)}) copy-start(f32[32,128]{1,0:T(8,128)} %constant.62.clone.refs_3_) | copy-start | bytes 49156
  0.1 41.0 %copy-start.1 = (s32[8]{0:T(128)S(1)}, s32[8]{0:T(128)}, u32[]{:S(2)}) copy-start(s32[8]{0:T(128)} %refs_0_.3) | copy-start | bytes 100
  0.1 41.0 %copy-start.2 = (f32[128]{0:T(128)S(1)}, f32[128]{0:T(128)}, u32[]{:S(2)}) copy-start(f32[128]{0:T(128)} %param.22) | copy-start | bytes 1540
  0.1 41.0 %copy-start = (f32[1,4096]{1,0:T(1,128)S(1)}, f32[1,4096]{1,0:T(1,128)}, u32[]{:S(2)}) copy-start(f32[1,4096]{1,0:T(1,128)} %param.21) | copy-start | bytes 49156
  0.1 15.7 %copy-start.15 = (s32[2,2,2048]{2,1,0:T(2,128)S(1)}, s32[2,2,2048]{2,1,0:T(2,128)}, u32[]{:S(2)}) copy-start(s32[2,2,2048]{2,1,0:T(2,128)} %param.25) | copy-start | bytes 98308
  0.2 15.8 %copy-start.14 = (f32[2,2048]{1,0:T(2,128)S(1)}, f32[2,2048]{1,0:T(2,128)}, u32[]{:S(2)}) copy-start(f32[2,2048]{1,0:T(2,128)} %param.24) | copy-start | bytes 49156
  5.8 18.7 %all-to-all-start = ((f32[16,64,128]{2,1,0:T(8,128)}), f32[16,64,128]{2,1,0:T(8,128)S(1)}, u32[]{:S(2)}, u32[]{:S(2)}) async-start(f32[16,64,128]{2,1,0:T(8,128)} %forward.1), calls=%async_computation | async-start | bytes 1048576 | tf_op jit(solution)/shard_map/all_to_all | solution.py:439
  16.0 7.0 %collective-permute-start = (f32[4,16,128]{2,1,0:T(8,128)S(1)}, f32[4,16,128]{2,1,0:T(8,128)S(1)}, u32[]{:S(2)}, u32[]{:S(2)}) collective-permute-start(f32[4,16,128]{2,1,0:T(8,128)S(1)} %bitcast.16), channel_id=1, source_target_pairs={{0,0},{1,1},{2,2},{3,3},{4,4},{5,5},{6,6},{7,7},{9,8},{8,9},{11,10... | collective-permute-start | bytes 98312 | tf_op jit(solution)/shard_map/ppermute | solution.py:456
  23.0 1.2 %collective-permute-start.1 = (f32[4,16,128]{2,1,0:T(8,128)S(1)}, f32[4,16,128]{2,1,0:T(8,128)S(1)}, u32[]{:S(2)}, u32[]{:S(2)}) collective-permute-start(f32[4,16,128]{2,1,0:T(8,128)S(1)} %collective-permute-done.src), channel_id=1, source_target_pairs={{0,8},{8,0},{16,24},{24,16},{32,40},{40,32},{48,56},{56,48},{64,72... | collective-permute-start | bytes 98312 | tf_op jit(solution)/shard_map/ppermute | solution.py:457
